TPU v7x, 256 devices: a whole 4x4x8 slice. The times are simulated.
256 devices in a mesh: bulk: 8 (over x, core), own: 32 (over y, z).
Axes of the slice: x: 4, y: 4, z: 8, core: 2. Of those that a mesh axis runs over, the one named last changes fastest.
Arguments:
- velocity: float32 [3, 8, 32, 96, 5832], P(None, 'bulk', 'own'), may hold values from -6 to 6
- new_owner: int32 [8, 32, 96], P('bulk', 'own'), may hold values from 0 to 31, as said below
- box_block: int32 [8, 32, 96], P('bulk', 'own'), may hold values from 0 to 383, as said below
- box_count: int32 [8, 32], P('bulk', 'own'), may hold values from 0 to 96, as said below
- box_level: int32 [8, 32, 96], P('bulk', 'own'), may hold values from 1 to 3
Outputs:
- cosine_part: float32 [32, 256, 3072], P('own', 'bulk')
- sine_part: float32 [32, 256, 3072], P('own', 'bulk')
Inputs may be any that keep to these rules, and one draw needn't show every extreme that they name: `new_owner`: at each bulk index b, the live slots that name new owner r number exactly 48 in all, and one old device gives either none or exactly 3 of them to one new owner. `box_block`: A live slot at bulk index b names a block from b * 48 to (b + 1) * 48 - 1, and the live slots at b that name one new owner name each of these blocks once. The live slots of an old device are its slots 0 to box_count - 1. At every bulk index some old device has all 96 slots live and some has none.
All inputs are finite; a program needn't handle non-finite values.
Results may differ from a plain program's by a relative error of at most 0.0003.
Values sent between devices are 32-bit elements; how exact they have to be, the bound alone decides.
A program may use at most 128 MiB of HBM per device.

v0:
```python
import math

import jax
import jax.numpy as jnp
from jax import lax
from jax.sharding import PartitionSpec as P

FA = 128
FB = 48
BOX = 16
HALF = 3072


HIGHEST = lax.Precision.HIGHEST


def level_factor(level):
    return jnp.where(level == 1, 0.5, jnp.where(level == 2, 1.0, 2.0)).astype(jnp.float32)


def cube_divergence(fields, factor):
    box_total = fields.shape[1]
    ghosted = BOX + 2
    cubes = fields.reshape(3, box_total, ghosted, ghosted, ghosted)
    streamwise = cubes[0]
    spanwise = cubes[1]
    vertical = cubes[2]
    along_x = streamwise[:, 1:-1, 1:-1, 2:] - streamwise[:, 1:-1, 1:-1, :-2]
    along_y = spanwise[:, 2:, 1:-1, 1:-1] - spanwise[:, :-2, 1:-1, 1:-1]
    along_z = vertical[:, 1:-1, 2:, 1:-1] - vertical[:, 1:-1, :-2, 1:-1]
    return factor[:, None, None, None] * (along_x + (along_y + along_z))


def angle_table(row_total, column_total, period):
    product = (
        jnp.arange(row_total, dtype=jnp.int32)[:, None]
        * jnp.arange(column_total, dtype=jnp.int32)[None, :]
        % period
    )
    angles = 2.0 * math.pi / period * product.astype(jnp.float32)
    return (jnp.cos(angles), jnp.sin(angles))


def line_spectra(pencil_rows):
    row_total = pencil_rows.shape[0]
    length = FA * FB
    blocks = pencil_rows.reshape(row_total, FB, FA)
    cos_one, sin_one = angle_table(FB, FB, FB)
    real_one = jnp.einsum("lbn,bq->lqn", blocks, cos_one, precision=HIGHEST)
    imag_one = -jnp.einsum("lbn,bq->lqn", blocks, sin_one, precision=HIGHEST)
    cos_twist, sin_twist = angle_table(FB, FA, length)
    real_two = real_one * cos_twist + imag_one * sin_twist
    imag_two = imag_one * cos_twist - real_one * sin_twist
    cos_last, sin_last = angle_table(FA, FA // 2, FA)
    real_out = jnp.einsum("lqn,nk->lkq", real_two, cos_last, precision=HIGHEST) + jnp.einsum(
        "lqn,nk->lkq", imag_two, sin_last, precision=HIGHEST
    )
    imag_out = jnp.einsum("lqn,nk->lkq", imag_two, cos_last, precision=HIGHEST) - jnp.einsum(
        "lqn,nk->lkq", real_two, sin_last, precision=HIGHEST
    )
    norm_scale = 1.0 / math.sqrt(length)
    cosine = real_out.reshape(row_total, HALF) * norm_scale
    sine_vals = -imag_out.reshape(row_total, HALF) * norm_scale
    return (cosine, sine_vals)


def body(velocity, new_owner, box_block, box_count, box_level):
    owners = lax.axis_size("own")
    groups = lax.axis_size("bulk")
    slot_total = velocity.shape[3]
    per_pair = slot_total // owners
    parcel_rows = owners * per_pair
    held_blocks = slot_total // 2
    first_block = lax.axis_index("bulk") * held_blocks
    slot_ids = jnp.arange(slot_total, dtype=jnp.int32)
    destination = new_owner[0, 0]
    filled = slot_ids < box_count[0, 0]
    owner_hits = (
        filled[:, None] & (destination[:, None] == jnp.arange(owners, dtype=jnp.int32)[None, :])
    ).astype(jnp.int32)
    earlier = jnp.cumsum(owner_hits, axis=0) - owner_hits
    order_rank = jnp.sum(earlier * owner_hits, axis=1)
    position = jnp.where(filled, destination * per_pair + order_rank, parcel_rows)
    source = jnp.full((parcel_rows,), slot_total, jnp.int32).at[position].set(slot_ids, mode="drop")
    occupied = source < slot_total
    source_safe = jnp.minimum(source, slot_total - 1)
    levels = jnp.where(occupied, jnp.take(box_level[0, 0], source_safe), 0).astype(jnp.float32)
    blocks_out = jnp.where(occupied, jnp.take(box_block[0, 0], source_safe), 0).astype(jnp.float32)
    arrived_ids = jnp.arange(parcel_rows, dtype=jnp.int32)
    parcel = jnp.where(
        occupied[None, :, None], jnp.take(velocity[:, 0, 0], source_safe, axis=1), 0.0
    )
    code_rows = jnp.stack([levels, blocks_out], axis=0)
    arrived_data, codes_in = (
        lax.all_to_all(parcel, "own", split_axis=1, concat_axis=1, tiled=True),
        lax.all_to_all(code_rows, "own", split_axis=1, concat_axis=1, tiled=True),
    )
    level_in = codes_in[0].astype(jnp.int32)
    place_at = jnp.where(level_in > 0, codes_in[1].astype(jnp.int32) - first_block, held_blocks)
    chosen = jnp.zeros((held_blocks,), jnp.int32).at[place_at].set(arrived_ids, mode="drop")
    fields = jnp.take(arrived_data, chosen, axis=1)
    column = cube_divergence(fields, level_factor(jnp.take(level_in, chosen)))
    pencil_rows = jnp.transpose(column, (1, 2, 0, 3)).reshape(
        groups, BOX * BOX // groups, held_blocks * BOX
    )
    cosine, sine_vals = line_spectra(
        lax.all_to_all(pencil_rows, "bulk", split_axis=0, concat_axis=2, tiled=True)[0]
    )
    cosine_part = cosine[None]
    sine_part = sine_vals[None]
    return (cosine_part, sine_part)


def solution(mesh):
    in_specs = (
        P(None, "bulk", "own", None, None),
        P("bulk", "own", None),
        P("bulk", "own", None),
        P("bulk", "own"),
        P("bulk", "own", None),
    )
    out_specs = (P("own", "bulk", None), P("own", "bulk", None))
    return jax.shard_map(body, mesh=mesh, in_specs=in_specs, out_specs=out_specs, check_vma=False)
```

profile of v0, /device:TPU:96, one launch (start us, length us, event | category | flops | bytes accessed | tf_op | source)
XLA Modules:
  0.0 361.3 jit_solution(88810560121162678)
XLA Ops:
  1.3 0.7 fusion.16
  2.1 0.1 reduce_window_sum.11
  2.2 0.8 select_reduce_fusion
  3.1 0.7 fusion.64
  3.7 0.9 scatter_custom_fusion
  4.7 1.2 gather_fusion.3
  5.9 1.6 gather_fusion.4
  7.5 0.1 stack.10
  7.6 0.1 stack.9
  7.7 0.6 copy.26
  8.4 10.4 %all-to-all-start = ((f32[2,32,3]{2,0,1:T(2,128)}), f32[2,32,3]{2,0,1:T(2,128)S(1)}, u32[]{:S(2)}, u32[]{:S(2)}) async-start(f32[2,32,3]{2,0,1:T(2,128)} %copy.26), calls=%async_computation | async-start | bytes 65536 | tf_op jit(solution)/shard_map/all_to_all | solution.py:96
  18.8 11.1 %copy.36 = f32[3,1,1,96,5832]{4,0,3,2,1:T(4,128)} copy(f32[3,1,1,96,5832]{4,3,2,1,0:T(8,128)} %param.7) | data formatting | bytes 13436928 | tf_op args[0]
  29.9 16.2 %gather_fusion.1 = f32[96,3,5832]{2,1,0:T(4,128)} fusion(f32[3,96,5832]{2,0,1:T(4,128)} %bitcast.76, s32[1024]{0:T(1024)S(1)} %pad_clamp_fusion.1), kind=kCustom, calls=%fused_computation.3 | custom fusion | bytes 13437312 | tf_op jit(solution)/shard_map/jit(_take)/gather | solution.py:91
  46.0 12.6 %select_bitcast_fusion = f32[3,96,5832]{2,0,1:T(4,128)} fusion(f32[96,3,5832]{2,1,0:T(4,128)} %gather_fusion.1, pred[96]{0:T(512)(128)(4,1)S(1)} %get-tuple-element.13, pred[96]{0:T(512)(128)(4,1)S(1)} %get-tuple-element.12), kind=kLoop, calls=%fused_computation.8 | loop fusion | flops 3359232 | bytes 13437120 | tf_op jit(solution)/shard_map/jit(_where)/select_n | solution.py:90
  58.6 9.9 %all-to-all-start.1 = ((f32[3,96,5832]{2,0,1:T(4,128)}), f32[3,96,5832]{2,0,1:T(4,128)}, u32[]{:S(2)}, u32[]{:S(2)}) async-start(f32[3,96,5832]{2,0,1:T(4,128)} %select_bitcast_fusion), calls=%async_computation.1 | async-start | bytes 18087936 | tf_op jit(solution)/shard_map/all_to_all | solution.py:95
  68.5 0.1 fusion.60
  68.6 0.1 select_n.145
  68.7 0.1 convert_element_type.71
  68.8 0.9 scatter_custom_fusion.1
  69.7 0.8 gather_fusion
  70.5 199.3 %all-to-all-done.1 = f32[3,96,5832]{2,0,1:T(4,128)} async-done(((f32[3,96,5832]{2,0,1:T(4,128)}), f32[3,96,5832]{2,0,1:T(4,128)}, u32[]{:S(2)}, u32[]{:S(2)}) %all-to-all-start.1) | async-done | bytes 6718496 | tf_op jit(solution)/shard_map/all_to_all | solution.py:95
  269.9 8.9 %gather_fusion.2 = f32[48,3,5832]{2,1,0:T(4,128)} fusion(f32[3,96,5832]{2,0,1:T(4,128)} %all-to-all-done.1, s32[1024]{0:T(1024)S(1)} %pad_clamp_fusion), kind=kCustom, calls=%fused_computation.4 | custom fusion | bytes 6718656 | tf_op jit(solution)/shard_map/jit(_take)/gather | solution.py:101
  278.8 3.4 select_bitcast_fusion.1
  282.2 4.2 %fusion.91 = (f32[1,48,5832]{2,0,1:T(1,128)}, f32[1,48,5832]{2,0,1:T(1,128)}, f32[1,48,5832]{2,0,1:T(1,128)}) fusion(f32[3,48,5832]{2,0,1:T(4,128)S(1)} %select_bitcast_fusion.1), kind=kLoop, calls=%fused_computation.130 | loop fusion | bytes 6718464 | tf_op jit(solution)/shard_map/slice | solution.py:25
  286.5 3.1 copy.30
  289.5 2.3 squeeze.30
  291.9 3.1 copy.29
  295.0 2.3 squeeze.29
  297.3 3.1 copy.28
  300.4 2.4 squeeze.28
  302.8 7.6 %fusion.3 = f32[16,16,48,16]{2,3,1,0:T(8,128)S(1)} fusion(f32[48,18,18,18]{0,3,2,1:T(8,128)} %squeeze.30, f32[48,18,18,18]{0,3,2,1:T(8,128)} %squeeze.29, f32[48,18,18,18]{0,3,2,1:T(8,128)} %squeeze.28, f32[48]{0:T(128)S(1)} %get-tuple-element.5), kind=kLoop, calls=%fused_computation.14 | loop fusion | flops 1179648 | bytes 5505216 | tf_op jit(solution)/shard_map/transpose | solution.py:103
  310.4 4.1 %copy.31 = f32[16,16,48,16]{3,2,1,0:T(8,128)} copy(f32[16,16,48,16]{2,3,1,0:T(8,128)S(1)} %fusion.3) | data formatting | bytes 1572864 | tf_op jit(solution)/shard_map/transpose | solution.py:103
  314.5 5.6 %reshape.200 = f32[8,32,768]{2,1,0:T(8,128)} reshape(f32[16,16,48,16]{3,2,1,0:T(8,128)} %copy.31) | data formatting | bytes 1572864 | tf_op jit(solution)/shard_map/reshape | solution.py:103
  320.1 16.4 %all-to-all-start.2 = ((f32[8,32,768]{2,1,0:T(8,128)}), f32[8,32,768]{2,1,0:T(8,128)S(1)}, u32[]{:S(2)}, u32[]{:S(2)}) async-start(f32[8,32,768]{2,1,0:T(8,128)} %reshape.200), calls=%async_computation.2 | async-start | bytes 1572864 | tf_op jit(solution)/shard_map/all_to_all | solution.py:107
  336.5 0.1 fusion.37
  336.6 13.0 %all-to-all-done.2 = f32[8,32,768]{2,1,0:T(8,128)S(1)} async-done(((f32[8,32,768]{2,1,0:T(8,128)}), f32[8,32,768]{2,1,0:T(8,128)S(1)}, u32[]{:S(2)}, u32[]{:S(2)}) %all-to-all-start.2) | async-done | bytes 786464 | tf_op jit(solution)/shard_map/all_to_all | solution.py:107
  349.7 0.5 copy.32
  350.1 0.1 reshape_squeeze.3
  350.2 0.9 convolution_negate_fusion
  351.1 0.9 fusion.32
  352.0 0.9 fusion.13
  352.9 1.8 fusion.9
  354.7 0.9 fusion.6
  355.7 0.3 copy.33
  356.0 1.4 mul.255
  357.5 2.1 fusion.8
  359.5 0.3 copy.34
  359.9 1.4 mul.258
  (17 shorter events, 0.1 us)
Async XLA Ops:
  0.6 4.0 %copy-start = (s32[1,1,96]{2,1,0:T(1,128)S(1)}, s32[1,1,96]{2,1,0:T(1,128)}, u32[]{:S(2)}) copy-start(s32[1,1,96]{2,1,0:T(1,128)} %param.11) | copy-start | bytes 1156
  8.4 50.2 %all-to-all-start = ((f32[2,32,3]{2,0,1:T(2,128)}), f32[2,32,3]{2,0,1:T(2,128)S(1)}, u32[]{:S(2)}, u32[]{:S(2)}) async-start(f32[2,32,3]{2,0,1:T(2,128)} %copy.26), calls=%async_computation | async-start | bytes 65536 | tf_op jit(solution)/shard_map/all_to_all | solution.py:96
  58.6 211.3 %all-to-all-start.1 = ((f32[3,96,5832]{2,0,1:T(4,128)}), f32[3,96,5832]{2,0,1:T(4,128)}, u32[]{:S(2)}, u32[]{:S(2)}) async-start(f32[3,96,5832]{2,0,1:T(4,128)} %select_bitcast_fusion), calls=%async_computation.1 | async-start | bytes 18087936 | tf_op jit(solution)/shard_map/all_to_all | solution.py:95
  320.1 29.5 %all-to-all-start.2 = ((f32[8,32,768]{2,1,0:T(8,128)}), f32[8,32,768]{2,1,0:T(8,128)S(1)}, u32[]{:S(2)}, u32[]{:S(2)}) async-start(f32[8,32,768]{2,1,0:T(8,128)} %reshape.200), calls=%async_computation.2 | async-start | bytes 1572864 | tf_op jit(solution)/shard_map/all_to_all | solution.py:107
  355.7 5.6 %copy-start.1 = (s32[1,1,96]{2,1,0:T(1,128)S(1)}, s32[1,1,96]{2,1,0:T(1,128)}, u32[]{:S(2)}) copy-start(s32[1,1,96]{2,1,0:T(1,128)} %param.11) | copy-start | bytes 1156
where the time goes:
time: 362 us; the launch traced here: 361 us
  waiting for transfers between devices  212 us (59%)
  local copies, waits for them, and re-layouts  76.9 us (21%)
  starting transfers between devices  36.7 us (10%)
  other arithmetic  26.3 us (7%)
  matrix products  7.5 us (2%)
    all_to_all x1, waiting for transfers between devices, body(): lax.all_to_all(parcel, 'own', split_axis=1, concat_axis=1, tiled=True)  199 us
    all_to_all x1, starting transfers between devices, body(): lax.all_to_all(pencil_rows, 'bulk', split_axis=0, concat_axis=2, tiled=True)  16.4 us
    gather x1, local copies, waits for them, and re-layouts, body(): jnp.take(velocity[:, 0, 0], source_safe, axis=1)  16.2 us
    all_to_all x1, waiting for transfers between devices, body(): lax.all_to_all(pencil_rows, 'bulk', split_axis=0, concat_axis=2, tiled=True)  13 us
    select_n x1, other arithmetic, body(): jnp.where(occupied[None, :, None], jnp.take(velocity[:, 0, 0], source_saf...  12.6 us
    unnamed x5, local copies, waits for them, and re-layouts  11.1 us
    all_to_all x1, starting transfers between devices, body(): lax.all_to_all(code_rows, 'own', split_axis=1, concat_axis=1, tiled=True)  10.4 us
    all_to_all x1, starting transfers between devices, body(): lax.all_to_all(parcel, 'own', split_axis=1, concat_axis=1, tiled=True)  9.86 us
  transfers between devices with their start and end apart: 3, of which 2 were waited for; matrix products, arithmetic and copies ran while one was open for 12% of the time, Pallas kernels for 0%

commit v1 on v0

v1 whole, which is shorter than its diff:
```python
import math

import numpy as np

import jax
import jax.numpy as jnp
from jax import lax
from jax.experimental import pallas as pl
from jax.experimental.pallas import tpu as pltpu
from jax.sharding import PartitionSpec as P

BOX = 16
GHOST = BOX + 2
PLANE = GHOST * GHOST
PLANE_PAD = 384
FACE = BOX * BOX
HALF = 3072
NX = 6144
SUB = 16
CODE_W = 256

HIGHEST = lax.Precision.HIGHEST
F32 = jnp.float32
BF16 = jnp.bfloat16


def level_factor(level):
    return jnp.where(level == 1, 0.5, jnp.where(level == 2, 1.0, 2.0)).astype(jnp.float32)


def stencil_tables():
    dx = np.zeros((PLANE_PAD, FACE), np.float32)
    dz = np.zeros((PLANE_PAD, FACE), np.float32)
    sel = np.zeros((PLANE_PAD, FACE), np.float32)
    for j in range(BOX):
        for k in range(BOX):
            q = j * BOX + k
            dx[GHOST * (j + 1) + k + 2, q] += 1.0
            dx[GHOST * (j + 1) + k, q] -= 1.0
            dz[GHOST * (j + 2) + k + 1, q] += 1.0
            dz[GHOST * j + k + 1, q] -= 1.0
            sel[GHOST * (j + 1) + k + 1, q] = 1.0
    return (jnp.asarray(dx, BF16), jnp.asarray(dz, BF16), jnp.asarray(sel, BF16))


def _split2(x):
    hi = x.astype(BF16)
    lo = (x - hi.astype(F32)).astype(BF16)
    return hi, lo


def _mm2(x, m):
    hi, lo = _split2(x)
    return jnp.dot(hi, m, preferred_element_type=F32) + jnp.dot(lo, m, preferred_element_type=F32)


def _mm3_left(p, x):
    hi = x.astype(BF16)
    rest = x - hi.astype(F32)
    mid = rest.astype(BF16)
    lo = (rest - mid.astype(F32)).astype(BF16)
    return (
        jnp.dot(p, hi, preferred_element_type=F32)
        + jnp.dot(p, mid, preferred_element_type=F32)
        + jnp.dot(p, lo, preferred_element_type=F32)
    )


def divergence_kernel(u_ref, w_ref, v0_ref, v2_ref, dx_ref, dz_ref, sel_ref, p_ref, code_ref, o_ref):
    i = pl.program_id(0)

    @pl.when(i < BOX)
    def _():
        along_x = _mm2(u_ref[0], dx_ref[...])
        along_y = _mm2(v2_ref[0] - v0_ref[0], sel_ref[...])
        along_z = _mm2(w_ref[0], dz_ref[...])
        o_ref[...] = _mm3_left(p_ref[...], along_x + (along_y + along_z))

    @pl.when(i == BOX)
    def _():
        o_ref[...] = code_ref[...]


def source_divergence(planes, permute, codes):
    slots = planes.shape[2]
    dx, dz, sel = stencil_tables()
    last = GHOST - 1
    plane_spec = lambda shift: pl.BlockSpec(
        (1, slots, PLANE_PAD), lambda i: (jnp.minimum(i + shift, last), 0, 0)
    )
    table_spec = pl.BlockSpec((PLANE_PAD, FACE), lambda i: (0, 0))
    return pl.pallas_call(
        divergence_kernel,
        grid=(BOX + 1,),
        in_specs=[
            plane_spec(1),
            plane_spec(1),
            plane_spec(0),
            plane_spec(2),
            table_spec,
            table_spec,
            table_spec,
            pl.BlockSpec((slots, slots), lambda i: (0, 0)),
            pl.BlockSpec((slots, CODE_W), lambda i: (0, 0)),
        ],
        out_specs=pl.BlockSpec((slots, FACE), lambda i: (0, i)),
        out_shape=jax.ShapeDtypeStruct((slots, (BOX + 1) * FACE), F32),
        cost_estimate=pl.CostEstimate(
            flops=2 * slots * PLANE_PAD * FACE * 6 * BOX + 2 * slots * slots * FACE * 3 * BOX,
            bytes_accessed=4 * (4 * BOX * slots * PLANE_PAD + slots * (BOX + 1) * FACE),
            transcendentals=0,
        ),
    )(planes[0], planes[2], planes[1], planes[1], dx, dz, sel, permute, codes)


def angle_cos_sin(product, period):
    angles = (2.0 * math.pi / period) * (product % period).astype(F32)
    return jnp.cos(angles), jnp.sin(angles)


def line_spectra(x):
    blocks, width = x.shape
    lines = width // SUB
    f2_total = HALF // blocks
    g_ids = jnp.arange(blocks, dtype=jnp.int32)
    c1, s1 = angle_cos_sin(g_ids[:, None] * g_ids[None, :], blocks)
    dims = (((0,), (0,)), ((), ()))
    y_re = lax.dot_general(x, c1, dims, precision=HIGHEST)
    y_im = -lax.dot_general(x, s1, dims, precision=HIGHEST)
    k_of = jnp.arange(width, dtype=jnp.int32) % SUB
    tw_c, tw_s = angle_cos_sin(k_of[:, None] * g_ids[None, :], NX)
    z_re = y_re * tw_c + y_im * tw_s
    z_im = y_im * tw_c - y_re * tw_s
    row = jnp.arange(lines * f2_total, dtype=jnp.int32)
    col = jnp.arange(width, dtype=jnp.int32)
    same_line = (row[:, None] // f2_total) == (col[None, :] // SUB)
    bd_c, bd_s = angle_cos_sin((row[:, None] % f2_total) * (col[None, :] % SUB), SUB)
    bd_c = jnp.where(same_line, bd_c, 0.0)
    bd_s = jnp.where(same_line, bd_s, 0.0)
    x_re = jnp.dot(bd_c, z_re, precision=HIGHEST) + jnp.dot(bd_s, z_im, precision=HIGHEST)
    x_im = jnp.dot(bd_c, z_im, precision=HIGHEST) - jnp.dot(bd_s, z_re, precision=HIGHEST)
    norm_scale = 1.0 / math.sqrt(NX)
    cosine = x_re.reshape(lines, HALF) * norm_scale
    sine_vals = -x_im.reshape(lines, HALF) * norm_scale
    return cosine, sine_vals


def body(velocity, new_owner, box_block, box_count, box_level):
    owners = lax.axis_size("own")
    groups = lax.axis_size("bulk")
    slot_total = velocity.shape[3]
    per_pair = slot_total // owners
    parcel_rows = owners * per_pair
    held_blocks = slot_total // 2
    first_block = lax.axis_index("bulk") * held_blocks
    slot_ids = jnp.arange(slot_total, dtype=jnp.int32)
    destination = new_owner[0, 0]
    filled = slot_ids < box_count[0, 0]
    owner_hits = (
        filled[:, None] & (destination[:, None] == jnp.arange(owners, dtype=jnp.int32)[None, :])
    ).astype(jnp.int32)
    earlier = jnp.cumsum(owner_hits, axis=0) - owner_hits
    order_rank = jnp.sum(earlier * owner_hits, axis=1)
    position = jnp.where(filled, destination * per_pair + order_rank, parcel_rows)
    parcel_ids = jnp.arange(parcel_rows, dtype=jnp.int32)
    factor = level_factor(box_level[0, 0])
    permute = jnp.where(position[None, :] == parcel_ids[:, None], factor[None, :], 0.0).astype(BF16)
    source = jnp.full((parcel_rows,), slot_total, jnp.int32).at[position].set(slot_ids, mode="drop")
    occupied = source < slot_total
    source_safe = jnp.minimum(source, slot_total - 1)
    blocks_out = jnp.where(occupied, jnp.take(box_block[0, 0], source_safe), -1).astype(F32)
    codes = jnp.broadcast_to(blocks_out[:, None], (parcel_rows, CODE_W))

    cells = velocity[:, 0, 0].reshape(3, slot_total, GHOST, PLANE)
    cells = jnp.pad(cells, ((0, 0), (0, 0), (0, 0), (0, PLANE_PAD - PLANE)))
    planes = jnp.transpose(cells, (0, 2, 1, 3))
    parcel = source_divergence(planes, permute, codes)

    arrived = lax.all_to_all(parcel, "own", split_axis=0, concat_axis=0, tiled=True)
    code_in = arrived[:, BOX * FACE]
    place_at = jnp.where(code_in >= 0, code_in.astype(jnp.int32) - first_block, held_blocks)
    chosen = jnp.zeros((held_blocks,), jnp.int32).at[place_at].set(parcel_ids, mode="drop")
    rows_per_group = BOX * FACE // groups
    column = arrived[:, : BOX * FACE].reshape(parcel_rows, groups, rows_per_group)
    outgoing = jnp.transpose(jnp.take(column, chosen, axis=0), (1, 0, 2))
    gathered = lax.all_to_all(outgoing, "bulk", split_axis=0, concat_axis=0, tiled=True)
    cosine, sine_vals = line_spectra(gathered.reshape(groups * held_blocks, rows_per_group))
    return (cosine[None], sine_vals[None])


def solution(mesh):
    in_specs = (
        P(None, "bulk", "own", None, None),
        P("bulk", "own", None),
        P("bulk", "own", None),
        P("bulk", "own"),
        P("bulk", "own", None),
    )
    out_specs = (P("own", "bulk", None), P("own", "bulk", None))
    return jax.shard_map(body, mesh=mesh, in_specs=in_specs, out_specs=out_specs, check_vma=False)
```

time: 362 us -> 159 us (0.44)
  the two profiles are of different devices: /device:TPU:96 before, /device:TPU:1 now
where the time goes in v1:
time: 159 us; the launch traced here: 158 us
  waiting for transfers between devices  63.8 us (40%)
  local copies, waits for them, and re-layouts  34 us (21%)
  matrix products  23.4 us (15%)
  starting transfers between devices  18.4 us (12%)
  Pallas kernels  16.1 us (10%)
    all_to_all x1, waiting for transfers between devices, body(): lax.all_to_all(parcel, 'own', split_axis=0, concat_axis=0, tiled=True)  51.5 us
    another operation x2, local copies, waits for them, and re-layouts, body(): cells = velocity[:, 0, 0].reshape(3, slot_total, GHOST, PLANE)  16.2 us
    pallas_call x1, Pallas kernels, source_divergence(): pl.pallas_call(divergence_kernel, grid=(BOX + 1,), in_specs=[plane_spec(1...  16.1 us
    all_to_all x1, waiting for transfers between devices, body(): lax.all_to_all(outgoing, 'bulk', split_axis=0, concat_axis=0, tiled=True)  12.3 us
    all_to_all x1, starting transfers between devices, body(): lax.all_to_all(parcel, 'own', split_axis=0, concat_axis=0, tiled=True)  12 us
    dot_general x1, matrix products, line_spectra(): y_re = lax.dot_general(x, c1, dims, precision=HIGHEST)  7.18 us
    all_to_all x1, starting transfers between devices, body(): lax.all_to_all(outgoing, 'bulk', split_axis=0, concat_axis=0, tiled=True)  6.44 us
    all_to_all x2, local copies, waits for them, and re-layouts, body(): lax.all_to_all(parcel, 'own', split_axis=0, concat_axis=0, tiled=True)  4.69 us
  transfers between devices with their start and end apart: 2, of which 2 were waited for; matrix products, arithmetic and copies ran while one was open for 0% of the time, Pallas kernels for 0%

profile of v1, /device:TPU:1, one launch (start us, length us, event | category | flops | bytes accessed | tf_op | source)
XLA Modules:
  0.0 158.4 jit_solution(14288418156989612040)
XLA Ops:
  0.6 0.0 copy-start
  0.6 10.8 %reshape_squeeze.3 = f32[3,96,18,324]{3,2,1,0:T(8,128)} reshape(f32[3,1,1,96,5832]{4,3,2,1,0:T(8,128)} %param.8) | data formatting | bytes 13436928 | tf_op jit(solution)/shard_map/reshape;squeeze | solution.py:174
  11.4 5.4 %copy.14 = f32[3,96,18,324]{3,1,2,0:T(8,128)S(1)} copy(f32[3,96,18,324]{3,2,1,0:T(8,128)} %reshape_squeeze.3) | data formatting | bytes 13436928 | tf_op jit(solution)/shard_map/reshape;squeeze | solution.py:174
  16.8 0.6 pad_bitcast_fusion
  17.4 0.0 copy-start.2
  17.4 0.0 copy-start.1
  17.4 3.3 %slice_bitcast_fusion = (f32[18,96,384]{2,1,0:T(8,128)}, f32[18,96,384]{2,1,0:T(8,128)}, f32[18,96,384]{2,1,0:T(8,128)}) fusion(f32[3,18,96,384]{3,2,1,0:T(8,128)S(1)} %pad_bitcast_fusion), kind=kLoop, calls=%fused_computation.5 | loop fusion | bytes 15925248 | tf_op jit(solution)/shard_map/squeeze | solution.py:113
  20.7 0.0 copy-done.2
  21.4 0.0 copy-done.1
  21.4 0.1 fusion.48
  21.5 0.1 reduce_window_sum.11
  21.6 0.2 select_reduce_fusion
  21.8 0.9 scatter_custom_fusion
  22.7 0.0 copy-done
  22.7 1.2 gather_fusion
  24.0 0.6 select_convert_fusion.p_ref
  24.6 0.7 broadcast_in_dim.99.code_ref
  25.3 16.1 %shard_map.95 = f32[96,4352]{1,0:T(8,128)} custom-call(f32[18,96,384]{2,1,0:T(8,128)} %get-tuple-element.4.u_ref, f32[18,96,384]{2,1,0:T(8,128)} %get-tuple-element.3.w_ref, f32[18,96,384]{2,1,0:T(8,128)} %get-tuple-element.2.v0_ref.v2_ref, f32[18,96,384]{2,1,0:T(8,128)} %get-tuple-element.2.v0_ref.v2_ref, bf16[384,256]{1,0:T(8,128)(2,1)} %constant.174.clone.dx_ref, ...), custom_call_target="tpu_custom_call" | custom-call | flops 2038431744 | bytes 11108352 | tf_op jit(solution)/shard_map/pallas_call | solution.py:92
  41.4 2.9 %all_to_all.11 = f32[32,3,4352]{2,1,0:T(4,128)} reshape(f32[96,4352]{1,0:T(8,128)} %shard_map.95) | data formatting | bytes 3342336 | tf_op jit(solution)/shard_map/all_to_all | solution.py:179
  44.3 12.0 %all-to-all-start = ((f32[32,3,4352]{2,1,0:T(4,128)}), f32[32,3,4352]{2,1,0:T(4,128)S(1)}, u32[]{:S(2)}, u32[]{:S(2)}) async-start(f32[32,3,4352]{2,1,0:T(4,128)} %all_to_all.11), calls=%async_computation | async-start | bytes 4456448 | tf_op jit(solution)/shard_map/all_to_all | solution.py:179
  56.3 51.5 %all-to-all-done = f32[32,3,4352]{2,1,0:T(4,128)S(1)} async-done(((f32[32,3,4352]{2,1,0:T(4,128)}), f32[32,3,4352]{2,1,0:T(4,128)S(1)}, u32[]{:S(2)}, u32[]{:S(2)}) %all-to-all-start) | async-done | bytes 1671200 | tf_op jit(solution)/shard_map/all_to_all | solution.py:179
  107.9 1.8 %all_to_all.13 = f32[96,4352]{1,0:T(8,128)} reshape(f32[32,3,4352]{2,1,0:T(4,128)S(1)} %all-to-all-done) | data formatting | bytes 3342336 | tf_op jit(solution)/shard_map/all_to_all | solution.py:179
  109.7 0.0 slice-start.1
  109.7 0.0 slice-start
  109.7 0.8 slice-done.1
  110.5 0.1 copy.17
  110.5 0.9 scatter_custom_fusion.1
  111.5 0.0 slice-done
  111.5 1.1 copy.18
  112.6 0.6 gather_fusion.1
  113.2 0.1 select_bitcast_fusion
  113.3 1.4 copy.16
  114.7 6.4 %all-to-all-start.1 = ((f32[8,48,512]{2,1,0:T(8,128)}), f32[8,48,512]{2,1,0:T(8,128)S(1)}, u32[]{:S(2)}, u32[]{:S(2)}) async-start(f32[8,48,512]{2,1,0:T(8,128)} %copy.16), calls=%async_computation.1 | async-start | bytes 1572864 | tf_op jit(solution)/shard_map/all_to_all | solution.py:186
  121.1 12.3 %all-to-all-done.1 = f32[8,48,512]{2,1,0:T(8,128)S(1)} async-done(((f32[8,48,512]{2,1,0:T(8,128)}), f32[8,48,512]{2,1,0:T(8,128)S(1)}, u32[]{:S(2)}, u32[]{:S(2)}) %all-to-all-start.1) | async-done | bytes 786464 | tf_op jit(solution)/shard_map/all_to_all | solution.py:186
  133.4 4.0 %convolution_negate_fusion = f32[512,384]{1,0:T(8,128)S(1)} fusion(f32[384,512]{1,0:T(8,128)S(1)} %bitcast.47), kind=kOutput, calls=%fused_computation.8 | convolution fusion | flops 907493376 | bytes 1572864 | tf_op jit(solution)/shard_map/dot_general | solution.py:129
  137.4 7.2 %multiply_subtract_fusion = (f32[512,384]{1,0:T(8,128)S(1)}, f32[512,384]{1,0:T(8,128)S(1)}) fusion(f32[512,384]{1,0:T(8,128)S(1)} %convolution_negate_fusion, s32[512]{0:T(512)S(1)} %get-tuple-element.7, f32[384,512]{1,0:T(8,128)S(1)} %bitcast.48), kind=kOutput, calls=%fused_computation.21 | convolution fusion | flops 910245888 | bytes 3147776 | tf_op jit(solution)/shard_map/dot_general | solution.py:128
  144.6 3.2 %fusion.24 = f32[256,384]{1,0:T(8,128)S(1)} fusion(f32[512,384]{1,0:T(8,128)S(1)} %get-tuple-element.6, s32[512]{0:T(512)S(1)} %get-tuple-element.7, s32[256]{0:T(256)S(1)} %get-tuple-element.9, s32[512]{0:T(512)S(1)} %get-tuple-element.8, s32[256]{0:T(256)S(1)} %get-tuple-element.10), kind=kOutput, calls=%fused_computation.47 | convolution fusion | flops 606076928 | bytes 1185792 | tf_op jit(solution)/shard_map/dot_general | solution.py:140
  147.8 3.0 %fusion.23 = f32[256,384]{1,0:T(8,128)S(1)} fusion(f32[512,384]{1,0:T(8,128)S(1)} %get-tuple-element.5, s32[512]{0:T(512)S(1)} %get-tuple-element.7, s32[256]{0:T(256)S(1)} %get-tuple-element.9, s32[512]{0:T(512)S(1)} %get-tuple-element.8, s32[256]{0:T(256)S(1)} %get-tuple-element.10), kind=kOutput, calls=%fused_computation.46 | convolution fusion | flops 606076928 | bytes 1185792 | tf_op jit(solution)/shard_map/dot_general | solution.py:141
  150.8 3.0 %fusion.1 = f32[256,384]{1,0:T(8,128)S(1)} fusion(f32[256,384]{1,0:T(8,128)S(1)} %fusion.24, f32[512,384]{1,0:T(8,128)S(1)} %get-tuple-element.5, s32[512]{0:T(512)S(1)} %get-tuple-element.7, s32[256]{0:T(256)S(1)} %get-tuple-element.9, s32[512]{0:T(512)S(1)} %get-tuple-element.8, s32[256]{0:T(256)S(1)} %get-tuple-element.10), kind=kOutput, calls=%fused_computation.12 | convolution fusion | flops 606273536 | bytes 1579008 | tf_op jit(solution)/shard_map/dot_general | solution.py:140
  153.8 0.8 mul.208
  154.6 3.0 %fusion.2 = f32[256,384]{1,0:T(8,128)S(1)} fusion(f32[256,384]{1,0:T(8,128)S(1)} %fusion.23, f32[512,384]{1,0:T(8,128)S(1)} %get-tuple-element.6, s32[512]{0:T(512)S(1)} %get-tuple-element.7, s32[256]{0:T(256)S(1)} %get-tuple-element.9, s32[512]{0:T(512)S(1)} %get-tuple-element.8, s32[256]{0:T(256)S(1)} %get-tuple-element.10), kind=kOutput, calls=%fused_computation.13 | convolution fusion | flops 606371840 | bytes 1579008 | tf_op jit(solution)/shard_map/dot_general | solution.py:141
  157.6 0.8 mul.210
  (15 shorter events, 0.1 us)
Async XLA Ops:
  0.6 22.1 %copy-start = (s32[1,1,96]{2,1,0:T(1,128)S(1)}, s32[1,1,96]{2,1,0:T(1,128)}, u32[]{:S(2)}) copy-start(s32[1,1,96]{2,1,0:T(1,128)} %param.10) | copy-start | bytes 1156
  17.4 3.3 %copy-start.2 = (s32[1,1,96]{2,1,0:T(1,128)S(1)}, s32[1,1,96]{2,1,0:T(1,128)}, u32[]{:S(2)}) copy-start(s32[1,1,96]{2,1,0:T(1,128)} %param.12) | copy-start | bytes 1156
  17.4 3.9 %copy-start.1 = (s32[1,1,96]{2,1,0:T(1,128)S(1)}, s32[1,1,96]{2,1,0:T(1,128)}, u32[]{:S(2)}) copy-start(s32[1,1,96]{2,1,0:T(1,128)} %param.9) | copy-start | bytes 1156
  44.3 63.5 %all-to-all-start = ((f32[32,3,4352]{2,1,0:T(4,128)}), f32[32,3,4352]{2,1,0:T(4,128)S(1)}, u32[]{:S(2)}, u32[]{:S(2)}) async-start(f32[32,3,4352]{2,1,0:T(4,128)} %all_to_all.11), calls=%async_computation | async-start | bytes 4456448 | tf_op jit(solution)/shard_map/all_to_all | solution.py:179
  109.7 0.8 slice-start.1
  109.7 1.8 %slice-start = ((f32[96,4352]{1,0:T(8,128)}), f32[96,4096]{1,0:T(8,128)S(1)}, s32[]{:S(2)}) async-start(f32[96,4352]{1,0:T(8,128)} %all_to_all.13), calls=%async_computation.2 | async-start | bytes 3145728 | tf_op jit(solution)/shard_map/slice | solution.py:184
  114.7 18.7 %all-to-all-start.1 = ((f32[8,48,512]{2,1,0:T(8,128)}), f32[8,48,512]{2,1,0:T(8,128)S(1)}, u32[]{:S(2)}, u32[]{:S(2)}) async-start(f32[8,48,512]{2,1,0:T(8,128)} %copy.16), calls=%async_computation.1 | async-start | bytes 1572864 | tf_op jit(solution)/shard_map/all_to_all | solution.py:186

commit v2 on v1

v2 whole, which is shorter than its diff:
```python
import math

import numpy as np

import jax
import jax.numpy as jnp
from jax import lax
from jax.experimental import pallas as pl
from jax.experimental.pallas import tpu as pltpu
from jax.sharding import PartitionSpec as P

BOX = 16
GHOST = BOX + 2
PLANE = GHOST * GHOST
PLANE_PAD = 384
FACE = BOX * BOX
HALF = 3072
NX = 6144
SUB = 16
CODE_W = 256

HIGHEST = lax.Precision.HIGHEST
F32 = jnp.float32
BF16 = jnp.bfloat16


def level_factor(level):
    return jnp.where(level == 1, 0.5, jnp.where(level == 2, 1.0, 2.0)).astype(jnp.float32)


def selection_table():
    sel = np.zeros((PLANE_PAD, FACE), np.float32)
    for j in range(BOX):
        for k in range(BOX):
            sel[GHOST * (j + 1) + k + 1, j * BOX + k] = 1.0
    return jnp.asarray(sel, BF16)


def _split2(x):
    hi = x.astype(BF16)
    lo = (x - hi.astype(F32)).astype(BF16)
    return hi, lo


def _split3(x):
    hi = x.astype(BF16)
    rest = x - hi.astype(F32)
    mid = rest.astype(BF16)
    lo = (rest - mid.astype(F32)).astype(BF16)
    return hi, mid, lo


def _dot(a, b):
    return jnp.dot(a, b, preferred_element_type=F32)


def _exact_right(x, m):
    hi, mid, lo = _split3(x)
    return _dot(hi, m) + _dot(mid, m) + _dot(lo, m)


def _exact_left(m, x):
    hi, mid, lo = _split3(x)
    return _dot(m, hi) + _dot(m, mid) + _dot(m, lo)


WINDOW = 512
ROW_PAD = 6016


def _plane(x_ref, field, p):
    start = PLANE * p
    base = (start // 128) * 128
    off = start - base
    w = x_ref[field, :, base:base + WINDOW]
    if off:
        w = pltpu.roll(w, WINDOW - off, 1)
    return w[:, :PLANE_PAD]


def divergence_kernel(x_ref, sel_ref, p_ref, code_ref, o_ref):
    h = pl.program_id(0)
    pieces = []
    for i in range(BOX):
        u = _plane(x_ref, 0, i + 1)
        w = _plane(x_ref, 2, i + 1)
        along_x = pltpu.roll(u, PLANE_PAD - 1, 1) - pltpu.roll(u, 1, 1)
        along_y = _plane(x_ref, 1, i + 2) - _plane(x_ref, 1, i)
        along_z = pltpu.roll(w, PLANE_PAD - GHOST, 1) - pltpu.roll(w, GHOST, 1)
        pieces.append(along_x + (along_y + along_z))
    interior = _exact_right(jnp.concatenate(pieces, axis=0), sel_ref[...])
    rows = p_ref.shape[2]
    permute = p_ref[0]

    @pl.when(h == 0)
    def _():
        o_ref[...] = jnp.zeros_like(o_ref)
        o_ref[:, BOX * FACE:] = code_ref[...]

    for i in range(BOX):
        o_ref[:, i * FACE:(i + 1) * FACE] += _exact_left(permute, interior[i * rows:(i + 1) * rows])


def source_divergence(flat, permute, codes, halves=2):
    slots = flat.shape[1]
    part = slots // halves
    sel = selection_table()
    return pl.pallas_call(
        divergence_kernel,
        grid=(halves,),
        in_specs=[
            pl.BlockSpec((3, part, ROW_PAD), lambda h: (0, h, 0)),
            pl.BlockSpec((PLANE_PAD, FACE), lambda h: (0, 0)),
            pl.BlockSpec((1, slots, part), lambda h: (h, 0, 0)),
            pl.BlockSpec((slots, CODE_W), lambda h: (0, 0)),
        ],
        out_specs=pl.BlockSpec((slots, BOX * FACE + CODE_W), lambda h: (0, 0)),
        out_shape=jax.ShapeDtypeStruct((slots, BOX * FACE + CODE_W), F32),
        cost_estimate=pl.CostEstimate(
            flops=2 * slots * BOX * PLANE_PAD * FACE * 3 + 2 * slots * slots * BOX * FACE * 3,
            bytes_accessed=4 * (3 * slots * ROW_PAD + slots * (BOX * FACE + CODE_W)),
            transcendentals=0,
        ),
    )(flat, sel, jnp.transpose(permute.reshape(slots, halves, part), (1, 0, 2)), codes)


def angle_cos_sin(product, period):
    angles = (2.0 * math.pi / period) * (product % period).astype(F32)
    return jnp.cos(angles), jnp.sin(angles)


def _split_table(t):
    hi = lax.reduce_precision(t, exponent_bits=8, mantissa_bits=7)
    return hi.astype(BF16), (t - hi).astype(BF16)


def _mm3(a_hi, a_lo, b_hi, b_lo, dims=None):
    if dims is None:
        f = _dot
    else:
        f = lambda a, b: lax.dot_general(a, b, dims, preferred_element_type=F32)
    return f(a_hi, b_hi) + (f(a_hi, b_lo) + f(a_lo, b_hi))


NT = (((1,), (1,)), ((), ()))


def dft_kernel(x_ref, c1h, c1l, s1h, s1l, twc_ref, tws_ref, bch, bcl, bsh, bsl, cos_ref, sin_ref):
    xh, xl = _split2(x_ref[...])
    y_re = _mm3(c1h[...], c1l[...], xh, xl)
    y_im = -_mm3(s1h[...], s1l[...], xh, xl)
    twc = twc_ref[...]
    tws = tws_ref[...]
    z_re = y_re * twc + y_im * tws
    z_im = y_im * twc - y_re * tws
    zrh, zrl = _split2(z_re)
    zih, zil = _split2(z_im)
    bc_h, bc_l, bs_h, bs_l = bch[...], bcl[...], bsh[...], bsl[...]
    x_re = _mm3(bc_h, bc_l, zrh, zrl, NT) + _mm3(bs_h, bs_l, zih, zil, NT)
    x_neg_im = _mm3(bs_h, bs_l, zrh, zrl, NT) - _mm3(bc_h, bc_l, zih, zil, NT)
    norm_scale = 1.0 / math.sqrt(NX)
    lines = cos_ref.shape[0]
    blocks = x_ref.shape[0]
    for f2 in range(cos_ref.shape[1] // blocks):
        cos_ref[:, f2 * blocks:(f2 + 1) * blocks] = x_re[f2 * lines:(f2 + 1) * lines] * norm_scale
        sin_ref[:, f2 * blocks:(f2 + 1) * blocks] = x_neg_im[f2 * lines:(f2 + 1) * lines] * norm_scale


def line_spectra(x):
    blocks, width = x.shape
    lines = width // SUB
    f2_total = HALF // blocks
    g_ids = jnp.arange(blocks, dtype=jnp.int32)
    c1, s1 = angle_cos_sin(g_ids[:, None] * g_ids[None, :], blocks)
    k_of = jnp.arange(width, dtype=jnp.int32) % SUB
    tw_c, tw_s = angle_cos_sin(g_ids[:, None] * k_of[None, :], NX)
    row = jnp.arange(lines * f2_total, dtype=jnp.int32)
    col = jnp.arange(width, dtype=jnp.int32)
    same_line = (row[:, None] % lines) == (col[None, :] // SUB)
    bd_c, bd_s = angle_cos_sin((row[:, None] // lines) * (col[None, :] % SUB), SUB)
    bd_c = jnp.where(same_line, bd_c, 0.0)
    bd_s = jnp.where(same_line, bd_s, 0.0)
    tables = (*_split_table(c1), *_split_table(s1), tw_c, tw_s, *_split_table(bd_c), *_split_table(bd_s))
    out = jax.ShapeDtypeStruct((lines, HALF), F32)
    return pl.pallas_call(
        dft_kernel,
        out_shape=(out, out),
        cost_estimate=pl.CostEstimate(
            flops=2 * 3 * (2 * blocks * blocks * width + 4 * lines * f2_total * width * blocks),
            bytes_accessed=4 * (blocks * width * 3 + 2 * lines * HALF) + 2 * (4 * blocks * blocks + 4 * lines * f2_total * width),
            transcendentals=0,
        ),
    )(x, *tables)


def body(velocity, new_owner, box_block, box_count, box_level):
    owners = lax.axis_size("own")
    groups = lax.axis_size("bulk")
    slot_total = velocity.shape[3]
    per_pair = slot_total // owners
    parcel_rows = owners * per_pair
    held_blocks = slot_total // 2
    first_block = lax.axis_index("bulk") * held_blocks
    slot_ids = jnp.arange(slot_total, dtype=jnp.int32)
    destination = new_owner[0, 0]
    filled = slot_ids < box_count[0, 0]
    owner_hits = (
        filled[:, None] & (destination[:, None] == jnp.arange(owners, dtype=jnp.int32)[None, :])
    ).astype(jnp.int32)
    earlier = jnp.cumsum(owner_hits, axis=0) - owner_hits
    order_rank = jnp.sum(earlier * owner_hits, axis=1)
    position = jnp.where(filled, destination * per_pair + order_rank, parcel_rows)
    parcel_ids = jnp.arange(parcel_rows, dtype=jnp.int32)
    factor = level_factor(box_level[0, 0])
    permute = jnp.where(position[None, :] == parcel_ids[:, None], factor[None, :], 0.0).astype(BF16)
    source = jnp.full((parcel_rows,), slot_total, jnp.int32).at[position].set(slot_ids, mode="drop")
    occupied = source < slot_total
    source_safe = jnp.minimum(source, slot_total - 1)
    blocks_out = jnp.where(occupied, jnp.take(box_block[0, 0], source_safe), -1).astype(F32)
    codes = jnp.broadcast_to(blocks_out[:, None], (parcel_rows, CODE_W))

    cells = velocity[:, 0, 0]
    flat = jnp.pad(cells, ((0, 0), (0, 0), (0, ROW_PAD - cells.shape[-1])))
    parcel = source_divergence(flat, permute, codes)

    arrived = lax.all_to_all(parcel, "own", split_axis=0, concat_axis=0, tiled=True)
    code_in = arrived[:, BOX * FACE]
    place_at = jnp.where(code_in >= 0, code_in.astype(jnp.int32) - first_block, held_blocks)
    chosen = jnp.zeros((held_blocks,), jnp.int32).at[place_at].set(parcel_ids, mode="drop")
    rows_per_group = BOX * FACE // groups
    column = arrived[:, : BOX * FACE].reshape(parcel_rows, groups, rows_per_group)
    outgoing = jnp.transpose(jnp.take(column, chosen, axis=0), (1, 0, 2))
    gathered = lax.all_to_all(outgoing, "bulk", split_axis=0, concat_axis=0, tiled=True)
    cosine, sine_vals = line_spectra(gathered.reshape(groups * held_blocks, rows_per_group))
    return (cosine[None], sine_vals[None])


def solution(mesh):
    in_specs = (
        P(None, "bulk", "own", None, None),
        P("bulk", "own", None),
        P("bulk", "own", None),
        P("bulk", "own"),
        P("bulk", "own", None),
    )
    out_specs = (P("own", "bulk", None), P("own", "bulk", None))
    return jax.shard_map(body, mesh=mesh, in_specs=in_specs, out_specs=out_specs, check_vma=False)
```

time: 159 us -> 128 us (0.81)
  matrix products: 23.4 us -> 0 us
  other arithmetic: 1.22 us -> 18.8 us
  local copies, waits for them, and re-layouts: 34 us -> 19.7 us
  waiting for transfers between devices: 63.8 us -> 49.6 us
  Pallas kernels: 16.1 us -> 20 us
    dot_general x6 -> x0, matrix products: 23.4 us -> none  [the longest x1 7.18 us: line_spectra(): y_re = lax.dot_general(x, c1, dims, precision=HIGHEST)]
    another operation x2 -> x0, local copies, waits for them, and re-layouts: 16.2 us -> none  [body(): cells = velocity[:, 0, 0].reshape(3, slot_total, GHOST, PLANE)]
    all_to_all x1, waiting for transfers between devices: 12.3 us -> 1.29 us  [body(): lax.all_to_all(outgoing, 'bulk', split_axis=0, concat_axis=0, tiled=True)]
    convert_element_type x0 -> x3, other arithmetic: none -> 9.85 us  [_split_table(): return (hi.astype(BF16), (t - hi).astype(BF16))]
    pad x0 -> x1, local copies, waits for them, and re-layouts: none -> 6.22 us  [body(): flat = jnp.pad(cells, ((0, 0), (0, 0), (0, ROW_PAD - cells.shape[-1])))]
    sin x0 -> x1, other arithmetic: none -> 4.37 us  [angle_cos_sin(): return (jnp.cos(angles), jnp.sin(angles))]
    pallas_call x1 -> x2, Pallas kernels: 16.1 us -> 20 us  [the longest x1 13.8 us: source_divergence(): pl.pallas_call(divergence_kernel, grid=(halves,), in_specs=[pl.BlockSpec(...]
    squeeze x1 -> x0, local copies, waits for them, and re-layouts: 3.25 us -> none  [source_divergence(): planes[1]]
  transfers between devices with their start and end apart: 2 -> 2, of which waited for: 2 -> 2; matrix products, arithmetic and copies ran while one was open for 0% -> 11% of each run, Pallas kernels for 0% -> 0%
where the time goes in v2:
time: 128 us
  waiting for transfers between devices  49.6 us (39%)
  Pallas kernels  20 us (16%)
  local copies, waits for them, and re-layouts  19.7 us (15%)
  other arithmetic  18.8 us (15%)
  starting transfers between devices  18.5 us (14%)
  between operations  1.47 us (1%)
    all_to_all x1, waiting for transfers between devices, body(): lax.all_to_all(parcel, 'own', split_axis=0, concat_axis=0, tiled=True)  48.3 us
    pallas_call x1, Pallas kernels, source_divergence(): pl.pallas_call(divergence_kernel, grid=(halves,), in_specs=[pl.BlockSpec(...  13.8 us
    all_to_all x1, starting transfers between devices, body(): lax.all_to_all(parcel, 'own', split_axis=0, concat_axis=0, tiled=True)  12 us
    convert_element_type x3, other arithmetic, _split_table(): return (hi.astype(BF16), (t - hi).astype(BF16))  9.85 us
    all_to_all x1, starting transfers between devices, body(): lax.all_to_all(outgoing, 'bulk', split_axis=0, concat_axis=0, tiled=True)  6.43 us
    pallas_call x1, Pallas kernels, line_spectra(): pl.pallas_call(dft_kernel, out_shape=(out, out), cost_estimate=pl.CostEst...  6.27 us
    pad x1, local copies, waits for them, and re-layouts, body(): flat = jnp.pad(cells, ((0, 0), (0, 0), (0, ROW_PAD - cells.shape[-1])))  6.22 us
    all_to_all x2, local copies, waits for them, and re-layouts, body(): lax.all_to_all(parcel, 'own', split_axis=0, concat_axis=0, tiled=True)  4.69 us
  transfers between devices with their start and end apart: 2, of which 2 were waited for; matrix products, arithmetic and copies ran while one was open for 11% of the time, Pallas kernels for 0%

profile of v2, /device:TPU:1, one launch (start us, length us, event | category | flops | bytes accessed | tf_op | source)
XLA Modules:
  0.0 128.1 jit_solution(15922503906320660424)
XLA Ops:
  0.6 0.0 copy-start
  1.3 0.7 multiply_reduce_fusion
  2.0 0.7 fusion.22
  2.7 0.1 reduce_window_sum.11
  2.9 0.8 select_reduce_fusion
  3.7 0.1 reduce_sum.14
  3.8 0.7 fusion.32
  4.5 0.9 scatter_custom_fusion
  5.4 0.0 copy-done
  5.4 1.2 gather_fusion
  6.7 0.1 mul.144
  6.7 0.7 fusion.29
  7.4 0.1 select_n.208
  7.5 0.6 select_convert_fusion.p_ref
  8.1 6.2 %pad.4.x_ref = f32[3,96,6016]{2,1,0:T(8,128)} pad(f32[3,96,5832]{2,1,0:T(8,128)} %bitcast.29, f32[]{:T(128)} %constant.141.clone.1), padding=0_0x0_0x0_184 | pad | bytes 13648900 | tf_op jit(solution)/shard_map/jit(_pad)/pad | solution.py:223
  14.4 0.7 broadcast_in_dim.105.code_ref
  15.1 13.8 %shard_map.77 = f32[96,4352]{1,0:T(8,128)} custom-call(f32[3,96,6016]{2,1,0:T(8,128)} %pad.4.x_ref, bf16[384,256]{1,0:T(8,128)(2,1)} %constant.167.clone.sel_ref, bf16[2,96,48]{2,1,0:T(8,128)(2,1)} %select_convert_fusion.p_ref, f32[96,256]{1,0:T(8,128)} %broadcast_in_dim.105.code_ref), custom_call_target="tpu_custom_call" | custom-call | flops 1132462080 | bytes 8601600 | tf_op jit(solution)/shard_map/pallas_call | solution.py:108
  28.9 2.9 %all_to_all.11 = f32[32,3,4352]{2,1,0:T(4,128)} reshape(f32[96,4352]{1,0:T(8,128)} %shard_map.77) | data formatting | bytes 3342336 | tf_op jit(solution)/shard_map/all_to_all | solution.py:226
  31.8 12.0 %all-to-all-start = ((f32[32,3,4352]{2,1,0:T(4,128)}), f32[32,3,4352]{2,1,0:T(4,128)S(1)}, u32[]{:S(2)}, u32[]{:S(2)}) async-start(f32[32,3,4352]{2,1,0:T(4,128)} %all_to_all.11), calls=%async_computation | async-start | bytes 4456448 | tf_op jit(solution)/shard_map/all_to_all | solution.py:226
  43.8 3.2 %reduce-precision_convert_fusion = (bf16[384,384]{1,0:T(8,128)(2,1)}, bf16[384,384]{1,0:T(8,128)(2,1)}) fusion(), kind=kLoop, calls=%fused_computation.10 | loop fusion | flops 1916928 | bytes 589824 | tf_op jit(solution)/shard_map/convert_element_type | solution.py:134
  47.1 48.3 %all-to-all-done = f32[32,3,4352]{2,1,0:T(4,128)S(1)} async-done(((f32[32,3,4352]{2,1,0:T(4,128)}), f32[32,3,4352]{2,1,0:T(4,128)S(1)}, u32[]{:S(2)}, u32[]{:S(2)}) %all-to-all-start) | async-done | bytes 1671200 | tf_op jit(solution)/shard_map/all_to_all | solution.py:226
  95.4 1.8 %all_to_all.13 = f32[96,4352]{1,0:T(8,128)} reshape(f32[32,3,4352]{2,1,0:T(4,128)S(1)} %all-to-all-done) | data formatting | bytes 3342336 | tf_op jit(solution)/shard_map/all_to_all | solution.py:226
  97.1 0.0 slice-start
  97.1 0.0 slice-start.1
  97.1 0.8 slice-done
  97.9 0.1 copy.13
  98.0 0.9 scatter_custom_fusion.1
  99.0 0.0 slice-done.1
  99.0 1.1 copy.14
  100.1 0.6 gather_fusion.1
  100.7 0.1 select_bitcast_fusion
  100.8 1.4 %copy.12 = f32[8,48,512]{2,1,0:T(8,128)} copy(f32[8,48,512]{2,0,1:T(8,128)S(1)} %select_bitcast_fusion) | data formatting | bytes 1572864 | tf_op jit(solution)/shard_map/jit(_take)/select_n | solution.py:232
  102.2 6.4 %all-to-all-start.1 = ((f32[8,48,512]{2,1,0:T(8,128)}), f32[8,48,512]{2,1,0:T(8,128)S(1)}, u32[]{:S(2)}, u32[]{:S(2)}) async-start(f32[8,48,512]{2,1,0:T(8,128)} %copy.12), calls=%async_computation.1 | async-start | bytes 1572864 | tf_op jit(solution)/shard_map/all_to_all | solution.py:233
  108.6 3.3 %fusion.7 = (bf16[384,384]{1,0:T(8,128)(2,1)}, bf16[384,384]{1,0:T(8,128)(2,1)}) fusion(), kind=kLoop, calls=%fused_computation.30 | loop fusion | flops 2211840 | bytes 589824 | tf_op jit(solution)/shard_map/convert_element_type | solution.py:134
  111.9 3.3 %fusion.17 = (bf16[256,512]{1,0:T(8,128)(2,1)}, bf16[256,512]{1,0:T(8,128)(2,1)}, bf16[256,512]{1,0:T(8,128)(2,1)}, bf16[256,512]{1,0:T(8,128)(2,1)}) fusion(s32[512]{0:T(512)S(1)} %get-tuple-element.13, s32[256]{0:T(256)S(1)} %get-tuple-element.14, s32[512]{0:T(512)S(1)} %get-tuple-element.12, s32[256]{0:T(256)S(1)} %get-tuple-element.15), kind=kLoop, calls=%fused_computation.41 | loop fusion | flops 3276800 | bytes 1054720 | tf_op jit(solution)/shard_map/convert_element_type | solution.py:134
  115.2 4.4 %fusion.4 = (f32[384,512]{1,0:T(8,128)}, f32[384,512]{1,0:T(8,128)}) fusion(s32[512]{0:T(512)S(1)} %get-tuple-element.13), kind=kLoop, calls=%fused_computation.20 | loop fusion | flops 1769472 | bytes 1574912 | tf_op jit(solution)/shard_map/sin | solution.py:129
  119.6 1.3 %all-to-all-done.1 = f32[8,48,512]{2,1,0:T(8,128)S(1)} async-done(((f32[8,48,512]{2,1,0:T(8,128)}), f32[8,48,512]{2,1,0:T(8,128)S(1)}, u32[]{:S(2)}, u32[]{:S(2)}) %all-to-all-start.1) | async-done | bytes 786464 | tf_op jit(solution)/shard_map/all_to_all | solution.py:233
  120.9 0.0 copy-start.1
  120.9 0.9 copy-done.1
  121.8 6.3 %shard_map.78 = (f32[32,3072]{1,0:T(8,128)}, f32[32,3072]{1,0:T(8,128)}) custom-call(f32[384,512]{1,0:T(8,128)} %bitcast.32, bf16[384,384]{1,0:T(8,128)(2,1)} %get-tuple-element.17.c1h, bf16[384,384]{1,0:T(8,128)(2,1)} %get-tuple-element.18.c1l, bf16[384,384]{1,0:T(8,128)(2,1)} %get-tuple-element.16.s1h, bf16[384,384]{1,0:T(8,128)(2,1)} %get-tuple-element.19.s1l, ...), custom_call_target="tpu_custom_call" | custom-call | flops 2113929216 | bytes 5373952 | tf_op jit(solution)/shard_map/pallas_call | solution.py:185
  (13 shorter events, 0.1 us)
Async XLA Ops:
  0.6 4.8 %copy-start = (s32[1,1,96]{2,1,0:T(1,128)S(1)}, s32[1,1,96]{2,1,0:T(1,128)}, u32[]{:S(2)}) copy-start(s32[1,1,96]{2,1,0:T(1,128)} %param.8) | copy-start | bytes 1156
  31.8 63.6 %all-to-all-start = ((f32[32,3,4352]{2,1,0:T(4,128)}), f32[32,3,4352]{2,1,0:T(4,128)S(1)}, u32[]{:S(2)}, u32[]{:S(2)}) async-start(f32[32,3,4352]{2,1,0:T(4,128)} %all_to_all.11), calls=%async_computation | async-start | bytes 4456448 | tf_op jit(solution)/shard_map/all_to_all | solution.py:226
  97.1 0.8 slice-start
  97.1 1.8 %slice-start.1 = ((f32[96,4352]{1,0:T(8,128)}), f32[96,4096]{1,0:T(8,128)S(1)}, s32[]{:S(2)}) async-start(f32[96,4352]{1,0:T(8,128)} %all_to_all.13), calls=%async_computation.3 | async-start | bytes 3145728 | tf_op jit(solution)/shard_map/slice | solution.py:231
  102.2 18.7 %all-to-all-start.1 = ((f32[8,48,512]{2,1,0:T(8,128)}), f32[8,48,512]{2,1,0:T(8,128)S(1)}, u32[]{:S(2)}, u32[]{:S(2)}) async-start(f32[8,48,512]{2,1,0:T(8,128)} %copy.12), calls=%async_computation.1 | async-start | bytes 1572864 | tf_op jit(solution)/shard_map/all_to_all | solution.py:233
  120.9 0.9 copy-start.1

commit v3 on v2

--- a/solution.py
+++ b/solution.py
@@ -1,5 +1,6 @@
 import math
 
+import ml_dtypes
 import numpy as np
 
 import jax
@@ -17,7 +18,7 @@
 HALF = 3072
 NX = 6144
 SUB = 16
-CODE_W = 256
+CODE_W = 128
 
 HIGHEST = lax.Precision.HIGHEST
 F32 = jnp.float32
@@ -124,14 +125,33 @@
     )(flat, sel, jnp.transpose(permute.reshape(slots, halves, part), (1, 0, 2)), codes)
 
 
-def angle_cos_sin(product, period):
-    angles = (2.0 * math.pi / period) * (product % period).astype(F32)
-    return jnp.cos(angles), jnp.sin(angles)
-
-
-def _split_table(t):
-    hi = lax.reduce_precision(t, exponent_bits=8, mantissa_bits=7)
-    return hi.astype(BF16), (t - hi).astype(BF16)
+def _split_np(t):
+    hi = t.astype(ml_dtypes.bfloat16)
+    lo = (t - hi.astype(np.float64)).astype(ml_dtypes.bfloat16)
+    return jnp.asarray(hi), jnp.asarray(lo)
+
+
+def _angles(product, period):
+    return (2.0 * np.pi / period) * (product % period).astype(np.float64)
+
+
+def dft_tables(blocks, lines_per_block, f2_total):
+    g_ids = np.arange(blocks, dtype=np.int64)
+    stage_one = _angles(g_ids[:, None] * g_ids[None, :], blocks)
+    lanes = lines_per_block * SUB
+    twist = _angles(g_ids[:, None] * (np.arange(lanes) % SUB)[None, :], NX)
+    row = np.arange(f2_total * lines_per_block)
+    col = np.arange(lanes)
+    same_line = (row[:, None] % lines_per_block) == (col[None, :] // SUB)
+    last = _angles((row[:, None] // lines_per_block) * (col[None, :] % SUB), SUB)
+    return (
+        *_split_np(np.cos(stage_one)),
+        *_split_np(np.sin(stage_one)),
+        jnp.asarray(np.cos(twist), F32),
+        jnp.asarray(np.sin(twist), F32),
+        *_split_np(np.where(same_line, np.cos(last), 0.0)),
+        *_split_np(np.where(same_line, np.sin(last), 0.0)),
+    )
 
 
 def _mm3(a_hi, a_lo, b_hi, b_lo, dims=None):
@@ -143,6 +163,7 @@
 
 
 NT = (((1,), (1,)), ((), ()))
+LANE = 128
 
 
 def dft_kernel(x_ref, c1h, c1l, s1h, s1l, twc_ref, tws_ref, bch, bcl, bsh, bsl, cos_ref, sin_ref):
@@ -151,43 +172,37 @@
     y_im = -_mm3(s1h[...], s1l[...], xh, xl)
     twc = twc_ref[...]
     tws = tws_ref[...]
-    z_re = y_re * twc + y_im * tws
-    z_im = y_im * twc - y_re * tws
-    zrh, zrl = _split2(z_re)
-    zih, zil = _split2(z_im)
     bc_h, bc_l, bs_h, bs_l = bch[...], bcl[...], bsh[...], bsl[...]
-    x_re = _mm3(bc_h, bc_l, zrh, zrl, NT) + _mm3(bs_h, bs_l, zih, zil, NT)
-    x_neg_im = _mm3(bs_h, bs_l, zrh, zrl, NT) - _mm3(bc_h, bc_l, zih, zil, NT)
     norm_scale = 1.0 / math.sqrt(NX)
-    lines = cos_ref.shape[0]
     blocks = x_ref.shape[0]
-    for f2 in range(cos_ref.shape[1] // blocks):
-        cos_ref[:, f2 * blocks:(f2 + 1) * blocks] = x_re[f2 * lines:(f2 + 1) * lines] * norm_scale
-        sin_ref[:, f2 * blocks:(f2 + 1) * blocks] = x_neg_im[f2 * lines:(f2 + 1) * lines] * norm_scale
+    lines_per_block = LANE // SUB
+    for part in range(x_ref.shape[1] // LANE):
+        cols = slice(part * LANE, (part + 1) * LANE)
+        yr = y_re[:, cols]
+        yi = y_im[:, cols]
+        zrh, zrl = _split2(yr * twc + yi * tws)
+        zih, zil = _split2(yi * twc - yr * tws)
+        x_re = _mm3(bc_h, bc_l, zrh, zrl, NT) + _mm3(bs_h, bs_l, zih, zil, NT)
+        x_neg_im = _mm3(bs_h, bs_l, zrh, zrl, NT) - _mm3(bc_h, bc_l, zih, zil, NT)
+        rows = slice(part * lines_per_block, (part + 1) * lines_per_block)
+        for f2 in range(cos_ref.shape[1] // blocks):
+            picked = slice(f2 * lines_per_block, (f2 + 1) * lines_per_block)
+            cos_ref[rows, f2 * blocks:(f2 + 1) * blocks] = x_re[picked] * norm_scale
+            sin_ref[rows, f2 * blocks:(f2 + 1) * blocks] = x_neg_im[picked] * norm_scale
 
 
 def line_spectra(x):
     blocks, width = x.shape
     lines = width // SUB
     f2_total = HALF // blocks
-    g_ids = jnp.arange(blocks, dtype=jnp.int32)
-    c1, s1 = angle_cos_sin(g_ids[:, None] * g_ids[None, :], blocks)
-    k_of = jnp.arange(width, dtype=jnp.int32) % SUB
-    tw_c, tw_s = angle_cos_sin(g_ids[:, None] * k_of[None, :], NX)
-    row = jnp.arange(lines * f2_total, dtype=jnp.int32)
-    col = jnp.arange(width, dtype=jnp.int32)
-    same_line = (row[:, None] % lines) == (col[None, :] // SUB)
-    bd_c, bd_s = angle_cos_sin((row[:, None] // lines) * (col[None, :] % SUB), SUB)
-    bd_c = jnp.where(same_line, bd_c, 0.0)
-    bd_s = jnp.where(same_line, bd_s, 0.0)
-    tables = (*_split_table(c1), *_split_table(s1), tw_c, tw_s, *_split_table(bd_c), *_split_table(bd_s))
+    tables = dft_tables(blocks, LANE // SUB, f2_total)
     out = jax.ShapeDtypeStruct((lines, HALF), F32)
     return pl.pallas_call(
         dft_kernel,
         out_shape=(out, out),
         cost_estimate=pl.CostEstimate(
-            flops=2 * 3 * (2 * blocks * blocks * width + 4 * lines * f2_total * width * blocks),
-            bytes_accessed=4 * (blocks * width * 3 + 2 * lines * HALF) + 2 * (4 * blocks * blocks + 4 * lines * f2_total * width),
+            flops=2 * 3 * (2 * blocks * blocks * width + 4 * f2_total * width * blocks * LANE // SUB),
+            bytes_accessed=4 * (blocks * width + 2 * lines * HALF + 2 * blocks * LANE) + 2 * 4 * blocks * blocks,
             transcendentals=0,
         ),
     )(x, *tables)

time: 128 us -> 124 us (0.969)
  blocking collectives: 0 us -> 18.8 us
  other arithmetic: 18.8 us -> 4.57 us
  starting transfers between devices: 18.5 us -> 12 us
  local copies, waits for them, and re-layouts: 19.7 us -> 17.8 us
    all_to_all x0 -> x1, blocking collectives: none -> 18.8 us  [body(): lax.all_to_all(outgoing, 'bulk', split_axis=0, concat_axis=0, tiled=True)]
    convert_element_type x3 -> x0, other arithmetic: 9.85 us -> none  [_split_table(): return (hi.astype(BF16), (t - hi).astype(BF16))]
    all_to_all x1 -> x0, starting transfers between devices: 6.43 us -> none  [body(): lax.all_to_all(outgoing, 'bulk', split_axis=0, concat_axis=0, tiled=True)]
    sin x1 -> x0, other arithmetic: 4.37 us -> none  [angle_cos_sin(): return (jnp.cos(angles), jnp.sin(angles))]
    all_to_all x1, waiting for transfers between devices: 48.3 us -> 50 us  [body(): lax.all_to_all(parcel, 'own', split_axis=0, concat_axis=0, tiled=True)]
    all_to_all x1 -> x0, waiting for transfers between devices: 1.29 us -> none  [body(): lax.all_to_all(outgoing, 'bulk', split_axis=0, concat_axis=0, tiled=True)]
  transfers between devices with their start and end apart: 2 -> 1, of which waited for: 2 -> 1; matrix products, arithmetic and copies ran while one was open for 11% -> 0% of each run, Pallas kernels for 0% -> 0%
where the time goes in v3:
time: 124 us
  waiting for transfers between devices  50 us (40%)
  Pallas kernels  19.4 us (16%)
  blocking collectives  18.8 us (15%)
  local copies, waits for them, and re-layouts  17.8 us (14%)
  starting transfers between devices  12 us (10%)
  other arithmetic  4.57 us (4%)
  between operations  1.46 us (1%)
    all_to_all x1, waiting for transfers between devices, body(): lax.all_to_all(parcel, 'own', split_axis=0, concat_axis=0, tiled=True)  50 us
    all_to_all x1, blocking collectives, body(): lax.all_to_all(outgoing, 'bulk', split_axis=0, concat_axis=0, tiled=True)  18.8 us
    pallas_call x1, Pallas kernels, source_divergence(): pl.pallas_call(divergence_kernel, grid=(halves,), in_specs=[pl.BlockSpec(...  13.7 us
    all_to_all x1, starting transfers between devices, body(): lax.all_to_all(parcel, 'own', split_axis=0, concat_axis=0, tiled=True)  12 us
    pad x1, local copies, waits for them, and re-layouts, body(): flat = jnp.pad(cells, ((0, 0), (0, 0), (0, ROW_PAD - cells.shape[-1])))  6.21 us
    pallas_call x1, Pallas kernels, line_spectra(): pl.pallas_call(dft_kernel, out_shape=(out, out), cost_estimate=pl.CostEst...  5.65 us
    all_to_all x2, local copies, waits for them, and re-layouts, body(): lax.all_to_all(parcel, 'own', split_axis=0, concat_axis=0, tiled=True)  4.6 us
  transfers between devices with their start and end apart: 1, of which 1 were waited for; matrix products, arithmetic and copies ran while one was open for 0% of the time, Pallas kernels for 0%

profile of v3, /device:TPU:1, one launch (start us, length us, event | category | flops | bytes accessed | tf_op | source)
XLA Modules:
  0.0 124.0 jit_solution(10230890133949104461)
XLA Ops:
  0.6 0.0 copy-start
  1.3 0.7 multiply_reduce_fusion
  2.0 0.7 fusion.1
  2.7 0.1 reduce_window_sum.11
  2.9 0.8 select_reduce_fusion
  3.7 0.1 reduce_sum.14
  3.8 0.7 fusion.5
  4.5 0.9 scatter_custom_fusion
  5.4 0.0 copy-done
  5.4 1.2 gather_fusion
  6.7 0.1 mul.31
  6.7 0.7 fusion.2
  7.4 0.1 select_n.89
  7.5 0.6 select_convert_fusion.p_ref
  8.1 6.2 %pad.4.x_ref = f32[3,96,6016]{2,1,0:T(8,128)} pad(f32[3,96,5832]{2,1,0:T(8,128)} %bitcast.29, f32[]{:T(128)} %constant.32.clone.1), padding=0_0x0_0x0_184 | pad | bytes 13648900 | tf_op jit(solution)/shard_map/jit(_pad)/pad | solution.py:238
  14.4 0.7 broadcast_in_dim.92.code_ref
  15.1 13.7 %shard_map.167 = f32[96,4224]{1,0:T(8,128)} custom-call(f32[3,96,6016]{2,1,0:T(8,128)} %pad.4.x_ref, bf16[384,256]{1,0:T(8,128)(2,1)} %constant.89.clone.sel_ref, bf16[2,96,48]{2,1,0:T(8,128)(2,1)} %select_convert_fusion.p_ref, f32[96,128]{1,0:T(8,128)} %broadcast_in_dim.92.code_ref), custom_call_target="tpu_custom_call" | custom-call | flops 1132462080 | bytes 8552448 | tf_op jit(solution)/shard_map/pallas_call | solution.py:109
  28.8 2.9 %all_to_all.11 = f32[32,3,4224]{2,1,0:T(4,128)} reshape(f32[96,4224]{1,0:T(8,128)} %shard_map.167) | data formatting | bytes 3244032 | tf_op jit(solution)/shard_map/all_to_all | solution.py:241
  31.6 12.0 %all-to-all-start = ((f32[32,3,4224]{2,1,0:T(4,128)}), f32[32,3,4224]{2,1,0:T(4,128)S(1)}, u32[]{:S(2)}, u32[]{:S(2)}) async-start(f32[32,3,4224]{2,1,0:T(4,128)} %all_to_all.11), calls=%async_computation | async-start | bytes 4325376 | tf_op jit(solution)/shard_map/all_to_all | solution.py:241
  43.7 50.0 %all-to-all-done = f32[32,3,4224]{2,1,0:T(4,128)S(1)} async-done(((f32[32,3,4224]{2,1,0:T(4,128)}), f32[32,3,4224]{2,1,0:T(4,128)S(1)}, u32[]{:S(2)}, u32[]{:S(2)}) %all-to-all-start) | async-done | bytes 1622048 | tf_op jit(solution)/shard_map/all_to_all | solution.py:241
  93.7 1.7 %all_to_all.13 = f32[96,4224]{1,0:T(8,128)} reshape(f32[32,3,4224]{2,1,0:T(4,128)S(1)} %all-to-all-done) | data formatting | bytes 3244032 | tf_op jit(solution)/shard_map/all_to_all | solution.py:241
  95.5 0.0 slice-start
  95.5 0.0 slice-start.1
  95.5 0.8 slice-done
  96.2 0.1 copy.23
  96.3 0.9 scatter_custom_fusion.1
  97.3 0.0 slice-done.1
  97.3 1.1 copy.24
  98.4 0.6 gather_fusion.1
  99.0 0.1 select_bitcast_fusion
  99.1 0.5 copy.22
  99.6 18.8 %all_to_all.17 = f32[8,48,512]{2,1,0:T(8,128)} all-to-all(f32[8,48,512]{2,1,0:T(8,128)S(1)} %copy.22), channel_id=1, replica_groups=mesh['bulk'=8,'own'=32] {'bulk'}, dimensions={0} | all-to-all | bytes 1572864 | tf_op jit(solution)/shard_map/all_to_all | solution.py:248
  118.3 5.6 %shard_map.168 = (f32[32,3072]{1,0:T(8,128)}, f32[32,3072]{1,0:T(8,128)}) custom-call(f32[384,512]{1,0:T(8,128)} %bitcast.32, bf16[384,384]{1,0:T(8,128)(2,1)} %constant.90.clone.c1h, bf16[384,384]{1,0:T(8,128)(2,1)} %constant.91.clone.c1l, bf16[384,384]{1,0:T(8,128)(2,1)} %constant.92.clone.s1h, bf16[384,384]{1,0:T(8,128)(2,1)} %constant.93.clone.s1l, ...), custom_call_target="tpu_custom_call" | custom-call | flops 1207959552 | bytes 3145728 | tf_op jit(solution)/shard_map/pallas_call | solution.py:200
  (11 shorter events, 0.1 us)
Async XLA Ops:
  0.6 4.8 %copy-start = (s32[1,1,96]{2,1,0:T(1,128)S(1)}, s32[1,1,96]{2,1,0:T(1,128)}, u32[]{:S(2)}) copy-start(s32[1,1,96]{2,1,0:T(1,128)} %param.18) | copy-start | bytes 1156
  31.6 62.1 %all-to-all-start = ((f32[32,3,4224]{2,1,0:T(4,128)}), f32[32,3,4224]{2,1,0:T(4,128)S(1)}, u32[]{:S(2)}, u32[]{:S(2)}) async-start(f32[32,3,4224]{2,1,0:T(4,128)} %all_to_all.11), calls=%async_computation | async-start | bytes 4325376 | tf_op jit(solution)/shard_map/all_to_all | solution.py:241
  95.5 0.8 slice-start
  95.5 1.8 %slice-start.1 = ((f32[96,4224]{1,0:T(8,128)}), f32[96,4096]{1,0:T(8,128)S(1)}, s32[]{:S(2)}) async-start(f32[96,4224]{1,0:T(8,128)} %all_to_all.13), calls=%async_computation.3 | async-start | bytes 3145728 | tf_op jit(solution)/shard_map/slice | solution.py:246

commit v4 on v3

--- a/solution.py
+++ b/solution.py
@@ -92,19 +92,33 @@
     interior = _exact_right(jnp.concatenate(pieces, axis=0), sel_ref[...])
     rows = p_ref.shape[2]
     permute = p_ref[0]
+    chunk_rows = o_ref.shape[0]
+    data_w = o_ref.shape[1] - code_ref.shape[1]
+    owners = code_ref.shape[0]
+    per_pair = permute.shape[0] // owners
+    groups = chunk_rows // owners
+    planes_per_group = BOX // groups
+    piece_w = data_w // per_pair
 
     @pl.when(h == 0)
     def _():
         o_ref[...] = jnp.zeros_like(o_ref)
-        o_ref[:, BOX * FACE:] = code_ref[...]
+        for g in range(groups):
+            o_ref[g * owners:(g + 1) * owners, data_w:] = code_ref[...]
 
     for i in range(BOX):
-        o_ref[:, i * FACE:(i + 1) * FACE] += _exact_left(permute, interior[i * rows:(i + 1) * rows])
-
-
-def source_divergence(flat, permute, codes, halves=2):
+        moved = _exact_left(permute, interior[i * rows:(i + 1) * rows])
+        g, half = divmod(i, planes_per_group)
+        for t in range(per_pair):
+            lane0 = t * piece_w + half * FACE
+            o_ref[g * owners:(g + 1) * owners, lane0:lane0 + FACE] += moved[t * owners:(t + 1) * owners]
+
+
+def source_divergence(flat, permute, codes, groups, halves=2):
     slots = flat.shape[1]
     part = slots // halves
+    owners = codes.shape[0]
+    out_w = BOX * FACE // groups * (slots // owners) + CODE_W
     sel = selection_table()
     return pl.pallas_call(
         divergence_kernel,
@@ -113,13 +127,13 @@
             pl.BlockSpec((3, part, ROW_PAD), lambda h: (0, h, 0)),
             pl.BlockSpec((PLANE_PAD, FACE), lambda h: (0, 0)),
             pl.BlockSpec((1, slots, part), lambda h: (h, 0, 0)),
-            pl.BlockSpec((slots, CODE_W), lambda h: (0, 0)),
+            pl.BlockSpec((owners, CODE_W), lambda h: (0, 0)),
         ],
-        out_specs=pl.BlockSpec((slots, BOX * FACE + CODE_W), lambda h: (0, 0)),
-        out_shape=jax.ShapeDtypeStruct((slots, BOX * FACE + CODE_W), F32),
+        out_specs=pl.BlockSpec((groups * owners, out_w), lambda h: (0, 0)),
+        out_shape=jax.ShapeDtypeStruct((groups * owners, out_w), F32),
         cost_estimate=pl.CostEstimate(
             flops=2 * slots * BOX * PLANE_PAD * FACE * 3 + 2 * slots * slots * BOX * FACE * 3,
-            bytes_accessed=4 * (3 * slots * ROW_PAD + slots * (BOX * FACE + CODE_W)),
+            bytes_accessed=4 * (3 * slots * ROW_PAD + groups * owners * out_w),
             transcendentals=0,
         ),
     )(flat, sel, jnp.transpose(permute.reshape(slots, halves, part), (1, 0, 2)), codes)
@@ -227,26 +241,33 @@
     position = jnp.where(filled, destination * per_pair + order_rank, parcel_rows)
     parcel_ids = jnp.arange(parcel_rows, dtype=jnp.int32)
     factor = level_factor(box_level[0, 0])
-    permute = jnp.where(position[None, :] == parcel_ids[:, None], factor[None, :], 0.0).astype(BF16)
+    row_of = jnp.where(filled, order_rank * owners + destination, parcel_rows)
+    permute = jnp.where(row_of[None, :] == parcel_ids[:, None], factor[None, :], 0.0).astype(BF16)
     source = jnp.full((parcel_rows,), slot_total, jnp.int32).at[position].set(slot_ids, mode="drop")
     occupied = source < slot_total
     source_safe = jnp.minimum(source, slot_total - 1)
     blocks_out = jnp.where(occupied, jnp.take(box_block[0, 0], source_safe), -1).astype(F32)
-    codes = jnp.broadcast_to(blocks_out[:, None], (parcel_rows, CODE_W))
+    code_lanes = jnp.arange(CODE_W, dtype=jnp.int32)
+    codes = jnp.where(
+        code_lanes[None, :] < per_pair,
+        jnp.take(blocks_out.reshape(owners, per_pair), jnp.minimum(code_lanes, per_pair - 1), axis=1),
+        0.0,
+    )
 
     cells = velocity[:, 0, 0]
     flat = jnp.pad(cells, ((0, 0), (0, 0), (0, ROW_PAD - cells.shape[-1])))
-    parcel = source_divergence(flat, permute, codes)
-
-    arrived = lax.all_to_all(parcel, "own", split_axis=0, concat_axis=0, tiled=True)
-    code_in = arrived[:, BOX * FACE]
-    place_at = jnp.where(code_in >= 0, code_in.astype(jnp.int32) - first_block, held_blocks)
-    chosen = jnp.zeros((held_blocks,), jnp.int32).at[place_at].set(parcel_ids, mode="drop")
-    rows_per_group = BOX * FACE // groups
-    column = arrived[:, : BOX * FACE].reshape(parcel_rows, groups, rows_per_group)
-    outgoing = jnp.transpose(jnp.take(column, chosen, axis=0), (1, 0, 2))
-    gathered = lax.all_to_all(outgoing, "bulk", split_axis=0, concat_axis=0, tiled=True)
-    cosine, sine_vals = line_spectra(gathered.reshape(groups * held_blocks, rows_per_group))
+    parcel = source_divergence(flat, permute, codes, groups)
+
+    arrived = lax.all_to_all(parcel, ("bulk", "own"), split_axis=0, concat_axis=0, tiled=True)
+    piece_w = BOX * FACE // groups
+    data_w = piece_w * per_pair
+    code_in = arrived[:, data_w:data_w + per_pair].reshape(-1)
+    total_blocks = groups * held_blocks
+    place_at = jnp.where(code_in >= 0, code_in.astype(jnp.int32), total_blocks)
+    arrived_ids = jnp.arange(code_in.shape[0], dtype=jnp.int32)
+    chosen = jnp.zeros((total_blocks,), jnp.int32).at[place_at].set(arrived_ids, mode="drop")
+    pieces = arrived[:, :data_w].reshape(-1, piece_w)
+    cosine, sine_vals = line_spectra(jnp.take(pieces, chosen, axis=0))
     return (cosine[None], sine_vals[None])
 
 

time: 124 us -> 109 us (0.88)
  waiting for transfers between devices: 50 us -> 0 us
  blocking collectives: 18.8 us -> 61.6 us
  starting transfers between devices: 12 us -> 0 us
  other arithmetic: 4.57 us -> 6.74 us
  local copies, waits for them, and re-layouts: 17.8 us -> 19.2 us
    all_to_all x1 -> x0, waiting for transfers between devices: 50 us -> none  [body(): lax.all_to_all(parcel, 'own', split_axis=0, concat_axis=0, tiled=True)]
    all_to_all x1, blocking collectives: 18.8 us -> 61.6 us  [body(): lax.all_to_all(parcel, ('bulk', 'own'), split_axis=0, concat_axis=0, tile...]
    all_to_all x1 -> x0, starting transfers between devices: 12 us -> none  [body(): lax.all_to_all(parcel, 'own', split_axis=0, concat_axis=0, tiled=True)]
    scatter x1, local copies, waits for them, and re-layouts: 0.88 us -> 3.55 us  [body(): jnp.zeros((total_blocks,), jnp.int32).at[place_at]]
    gather x1 -> x3, local copies, waits for them, and re-layouts: 0.61 us -> 2.34 us  [the longest x1 1.62 us: body(): cosine, sine_vals = line_spectra(jnp.take(pieces, chosen, axis=0))]
    select_n x4 -> x6, other arithmetic: 0.14 us -> 1.66 us  [the longest x2 1.01 us: body(): cosine, sine_vals = line_spectra(jnp.take(pieces, chosen, axis=0))]
    all_to_all x2 -> x1, local copies, waits for them, and re-layouts: 4.6 us -> 3.21 us  [body(): lax.all_to_all(parcel, ('bulk', 'own'), split_axis=0, concat_axis=0, tile...]
    unnamed x0 -> x1, other arithmetic: none -> 1.32 us
  transfers between devices with their start and end apart: 1 -> 0, of which waited for: 1 -> 0; matrix products, arithmetic and copies ran while one was open for 0% -> 0% of each run, Pallas kernels for 0% -> 0%
where the time goes in v4:
time: 109 us; the launch traced here: 108 us
  blocking collectives  61.6 us (57%)
  Pallas kernels  19.4 us (18%)
  local copies, waits for them, and re-layouts  19.2 us (18%)
  other arithmetic  6.74 us (6%)
  between operations  1.47 us (1%)
    all_to_all x1, blocking collectives, body(): lax.all_to_all(parcel, ('bulk', 'own'), split_axis=0, concat_axis=0, tile...  61.6 us
    pallas_call x1, Pallas kernels, source_divergence(): pl.pallas_call(divergence_kernel, grid=(halves,), in_specs=[pl.BlockSpec(...  13.8 us
    pad x1, local copies, waits for them, and re-layouts, body(): flat = jnp.pad(cells, ((0, 0), (0, 0), (0, ROW_PAD - cells.shape[-1])))  6.21 us
    pallas_call x1, Pallas kernels, line_spectra(): pl.pallas_call(dft_kernel, out_shape=(out, out), cost_estimate=pl.CostEst...  5.65 us
    scatter x1, local copies, waits for them, and re-layouts, body(): jnp.zeros((total_blocks,), jnp.int32).at[place_at]  3.55 us
    all_to_all x1, local copies, waits for them, and re-layouts, body(): lax.all_to_all(parcel, ('bulk', 'own'), split_axis=0, concat_axis=0, tile...  3.21 us

profile of v4, /device:TPU:1, one launch (start us, length us, event | category | flops | bytes accessed | tf_op | source)
XLA Modules:
  0.0 108.5 jit_solution(3090028752713295873)
XLA Ops:
  0.6 0.0 copy-start
  1.3 0.7 fusion.1
  2.1 0.1 reduce_window_sum.11
  2.2 0.8 select_reduce_fusion
  3.1 0.7 fusion.7
  3.8 0.9 scatter_custom_fusion
  4.7 0.0 copy-done
  4.7 1.2 %gather_fusion = s32[96]{0:T(128)S(1)} fusion(s32[96]{0:T(128)S(1)} %bitcast.29, s32[1024]{0:T(1024)S(1)} %pad_clamp_fusion.2), kind=kCustom, calls=%fused_computation | custom fusion | bytes 1152 | tf_op jit(solution)/shard_map/jit(_take)/gather | solution.py:249
  5.9 0.1 reshape.167
  6.0 0.1 copy.22
  6.1 0.7 gather_fusion.1
  6.8 0.1 copy.23
  6.8 0.1 mul.35
  6.9 0.5 broadcast.193
  7.4 1.3 %reduce.9 = s32[96]{0:T(128)S(1)} reduce(s32[1,1,96]{2,1,0:T(1,128)} %param.17, s32[]{:T(128)} %broadcast.193), dimensions={0,1}, to_apply=%param.17.reduce_sub_computation.3 | reduce | bytes 772 | tf_op args[1]
  8.7 0.1 squeeze.15
  8.8 0.7 fusion.5
  9.5 0.1 select_n.113
  9.6 0.6 select_convert_fusion.p_ref
  10.2 6.2 %pad.4.x_ref = f32[3,96,6016]{2,1,0:T(8,128)} pad(f32[3,96,5832]{2,1,0:T(8,128)} %bitcast.33, f32[]{:T(128)} %constant.38.clone.1), padding=0_0x0_0x0_184 | pad | bytes 13648900 | tf_op jit(solution)/shard_map/jit(_pad)/pad | solution.py:258
  16.5 0.6 select_bitcast_fusion.code_ref
  17.1 13.8 %shard_map.167 = f32[256,1664]{1,0:T(8,128)} custom-call(f32[3,96,6016]{2,1,0:T(8,128)} %pad.4.x_ref, bf16[384,256]{1,0:T(8,128)(2,1)} %constant.105.clone.sel_ref, bf16[2,96,48]{2,1,0:T(8,128)(2,1)} %select_convert_fusion.p_ref, f32[32,128]{1,0:T(8,128)} %select_bitcast_fusion.code_ref), custom_call_target="tpu_custom_call" | custom-call | flops 1132462080 | bytes 8634368 | tf_op jit(solution)/shard_map/pallas_call | solution.py:123
  30.8 3.2 %copy.24 = f32[256,1,1664]{2,1,0:T(1,128)S(1)} copy(f32[256,1,1664]{2,0,1:T(8,128)} %bitcast.32) | data formatting | bytes 3407872 | tf_op jit(solution)/shard_map/all_to_all | solution.py:261
  34.0 61.6 %all_to_all.12 = f32[256,1,1664]{2,1,0:T(1,128)S(1)} all-to-all(f32[256,1,1664]{2,1,0:T(1,128)S(1)} %copy.24), channel_id=1, replica_groups=mesh['bulk'=8,'own'=32] {'bulk','own'}, dimensions={0} | all-to-all | bytes 3407872 | tf_op jit(solution)/shard_map/all_to_all | solution.py:261
  95.7 0.1 copy.27
  95.8 0.2 slice.15
  96.0 0.2 select_n.123
  96.2 3.5 %scatter_custom_fusion.1 = s32[384]{0:T(512)S(1)} fusion(s32[768]{0:T(1024)S(1)} %fusion.2, s32[768]{0:T(1024)S(1)} %iota.60, s32[]{:T(128)} %constant.37.clone.1), kind=kCustom, calls=%fused_computation.30 | custom fusion | bytes 1540 | tf_op jit(solution)/shard_map/scatter | solution.py:268
  99.8 0.3 reshape.168
  100.2 1.6 %gather_fusion.2 = f32[384,512]{1,0:T(8,128)S(1)} fusion(f32[768,512]{1,0:T(8,128)S(1)} %reshape.168, s32[1024]{0:T(1024)S(1)} %pad_clamp_fusion), kind=kCustom, calls=%fused_computation.2 | custom fusion | bytes 1574400 | tf_op jit(solution)/shard_map/jit(_take)/gather | solution.py:270
  101.8 1.0 broadcast_select_fusion.x_ref
  102.8 5.6 %shard_map.168 = (f32[32,3072]{1,0:T(8,128)}, f32[32,3072]{1,0:T(8,128)}) custom-call(f32[384,512]{1,0:T(8,128)} %broadcast_select_fusion.x_ref, bf16[384,384]{1,0:T(8,128)(2,1)} %constant.106.clone.c1h, bf16[384,384]{1,0:T(8,128)(2,1)} %constant.107.clone.c1l, bf16[384,384]{1,0:T(8,128)(2,1)} %constant.108.clone.s1h, bf16[384,384]{1,0:T(8,128)(2,1)} %constant.109.clone.s1l, ...), custom_call_target="tpu_custom_call" | custom-call | flops 1207959552 | bytes 3145728 | tf_op jit(solution)/shard_map/pallas_call | solution.py:214
  (16 shorter events, 0.1 us)
Async XLA Ops:
  0.6 4.0 %copy-start = (s32[1,1,96]{2,1,0:T(1,128)S(1)}, s32[1,1,96]{2,1,0:T(1,128)}, u32[]{:S(2)}) copy-start(s32[1,1,96]{2,1,0:T(1,128)} %param.18) | copy-start | bytes 1156

commit v5 on v4

--- a/solution.py
+++ b/solution.py
@@ -79,64 +79,79 @@
     return w[:, :PLANE_PAD]
 
 
-def divergence_kernel(x_ref, sel_ref, p_ref, code_ref, o_ref):
-    h = pl.program_id(0)
-    pieces = []
-    for i in range(BOX):
-        u = _plane(x_ref, 0, i + 1)
-        w = _plane(x_ref, 2, i + 1)
-        along_x = pltpu.roll(u, PLANE_PAD - 1, 1) - pltpu.roll(u, 1, 1)
-        along_y = _plane(x_ref, 1, i + 2) - _plane(x_ref, 1, i)
-        along_z = pltpu.roll(w, PLANE_PAD - GHOST, 1) - pltpu.roll(w, GHOST, 1)
-        pieces.append(along_x + (along_y + along_z))
-    interior = _exact_right(jnp.concatenate(pieces, axis=0), sel_ref[...])
-    rows = p_ref.shape[2]
-    permute = p_ref[0]
+def divergence_kernel(src_ref, x_hbm, sel_ref, fac_ref, code_ref, o_ref, buf, sem):
+    owners = code_ref.shape[0]
+    per_pair = src_ref.shape[0] // owners
     chunk_rows = o_ref.shape[0]
     data_w = o_ref.shape[1] - code_ref.shape[1]
-    owners = code_ref.shape[0]
-    per_pair = permute.shape[0] // owners
     groups = chunk_rows // owners
     planes_per_group = BOX // groups
     piece_w = data_w // per_pair
 
-    @pl.when(h == 0)
-    def _():
-        o_ref[...] = jnp.zeros_like(o_ref)
-        for g in range(groups):
-            o_ref[g * owners:(g + 1) * owners, data_w:] = code_ref[...]
-
-    for i in range(BOX):
-        moved = _exact_left(permute, interior[i * rows:(i + 1) * rows])
-        g, half = divmod(i, planes_per_group)
-        for t in range(per_pair):
+    def fetch(t, slot):
+        for r in range(owners):
+            pltpu.make_async_copy(
+                x_hbm.at[:, pl.ds(src_ref[t * owners + r], 1), :],
+                buf.at[slot, :, pl.ds(r, 1), :],
+                sem.at[slot],
+            ).start()
+
+    def wait(slot):
+        pltpu.make_async_copy(x_hbm.at[:, pl.ds(0, owners), :], buf.at[slot], sem.at[slot]).wait()
+
+    fetch(0, 0)
+    for g in range(groups):
+        o_ref[g * owners:(g + 1) * owners, data_w:] = code_ref[...]
+    sel = sel_ref[...]
+    for t in range(per_pair):
+        slot = t % 2
+        if t + 1 < per_pair:
+            fetch(t + 1, 1 - slot)
+        wait(slot)
+        x_ref = buf.at[slot]
+        pieces = []
+        for i in range(BOX):
+            u = _plane(x_ref, 0, i + 1)
+            w = _plane(x_ref, 2, i + 1)
+            along_x = pltpu.roll(u, PLANE_PAD - 1, 1) - pltpu.roll(u, 1, 1)
+            along_y = _plane(x_ref, 1, i + 2) - _plane(x_ref, 1, i)
+            along_z = pltpu.roll(w, PLANE_PAD - GHOST, 1) - pltpu.roll(w, GHOST, 1)
+            pieces.append(along_x + (along_y + along_z))
+        interior = _exact_right(jnp.concatenate(pieces, axis=0), sel)
+        fac = fac_ref[t * owners:(t + 1) * owners, :]
+        for i in range(BOX):
+            g, half = divmod(i, planes_per_group)
             lane0 = t * piece_w + half * FACE
-            o_ref[g * owners:(g + 1) * owners, lane0:lane0 + FACE] += moved[t * owners:(t + 1) * owners]
-
-
-def source_divergence(flat, permute, codes, groups, halves=2):
+            o_ref[g * owners:(g + 1) * owners, lane0:lane0 + FACE] = interior[i * owners:(i + 1) * owners] * fac
+
+
+def source_divergence(flat, source, factor, codes, groups):
     slots = flat.shape[1]
-    part = slots // halves
     owners = codes.shape[0]
     out_w = BOX * FACE // groups * (slots // owners) + CODE_W
     sel = selection_table()
+    vmem = pl.BlockSpec(memory_space=pltpu.VMEM)
     return pl.pallas_call(
         divergence_kernel,
-        grid=(halves,),
         in_specs=[
-            pl.BlockSpec((3, part, ROW_PAD), lambda h: (0, h, 0)),
-            pl.BlockSpec((PLANE_PAD, FACE), lambda h: (0, 0)),
-            pl.BlockSpec((1, slots, part), lambda h: (h, 0, 0)),
-            pl.BlockSpec((owners, CODE_W), lambda h: (0, 0)),
+            pl.BlockSpec(memory_space=pltpu.SMEM),
+            pl.BlockSpec(memory_space=pl.ANY),
+            vmem,
+            vmem,
+            vmem,
         ],
-        out_specs=pl.BlockSpec((groups * owners, out_w), lambda h: (0, 0)),
+        out_specs=vmem,
         out_shape=jax.ShapeDtypeStruct((groups * owners, out_w), F32),
+        scratch_shapes=[
+            pltpu.VMEM((2, 3, owners, flat.shape[2]), F32),
+            pltpu.SemaphoreType.DMA((2,)),
+        ],
         cost_estimate=pl.CostEstimate(
-            flops=2 * slots * BOX * PLANE_PAD * FACE * 3 + 2 * slots * slots * BOX * FACE * 3,
+            flops=2 * slots * BOX * PLANE_PAD * FACE * 3,
             bytes_accessed=4 * (3 * slots * ROW_PAD + groups * owners * out_w),
             transcendentals=0,
         ),
-    )(flat, sel, jnp.transpose(permute.reshape(slots, halves, part), (1, 0, 2)), codes)
+    )(source, flat, sel, jnp.broadcast_to(factor[:, None], (slots, FACE)), codes)
 
 
 def _split_np(t):
@@ -241,8 +256,6 @@
     position = jnp.where(filled, destination * per_pair + order_rank, parcel_rows)
     parcel_ids = jnp.arange(parcel_rows, dtype=jnp.int32)
     factor = level_factor(box_level[0, 0])
-    row_of = jnp.where(filled, order_rank * owners + destination, parcel_rows)
-    permute = jnp.where(row_of[None, :] == parcel_ids[:, None], factor[None, :], 0.0).astype(BF16)
     source = jnp.full((parcel_rows,), slot_total, jnp.int32).at[position].set(slot_ids, mode="drop")
     occupied = source < slot_total
     source_safe = jnp.minimum(source, slot_total - 1)
@@ -253,10 +266,12 @@
         jnp.take(blocks_out.reshape(owners, per_pair), jnp.minimum(code_lanes, per_pair - 1), axis=1),
         0.0,
     )
+    row_factor = jnp.where(occupied, jnp.take(factor, source_safe), 0.0)
+    by_rank = lambda v: v.reshape(owners, per_pair).T.reshape(-1)
 
     cells = velocity[:, 0, 0]
     flat = jnp.pad(cells, ((0, 0), (0, 0), (0, ROW_PAD - cells.shape[-1])))
-    parcel = source_divergence(flat, permute, codes, groups)
+    parcel = source_divergence(flat, by_rank(source_safe), by_rank(row_factor), codes, groups)
 
     arrived = lax.all_to_all(parcel, ("bulk", "own"), split_axis=0, concat_axis=0, tiled=True)
     piece_w = BOX * FACE // groups

time: 109 us -> 110 us (level)
  local copies, waits for them, and re-layouts: 19.2 us -> 21.3 us
  other arithmetic: 6.74 us -> 4.77 us
    unnamed x1 -> x0, other arithmetic: 1.32 us -> none
    gather x0 -> x1, local copies, waits for them, and re-layouts: none -> 1.22 us  [body(): row_factor = jnp.where(occupied, jnp.take(factor, source_safe), 0.0)]
where the time goes in v5:
time: 110 us
  blocking collectives  62.6 us (57%)
  local copies, waits for them, and re-layouts  21.3 us (19%)
  Pallas kernels  19.9 us (18%)
  other arithmetic  4.77 us (4%)
  between operations  1.5 us (1%)
    all_to_all x1, blocking collectives, body(): lax.all_to_all(parcel, ('bulk', 'own'), split_axis=0, concat_axis=0, tile...  62.6 us
    pallas_call x1, Pallas kernels, source_divergence(): pl.pallas_call(divergence_kernel, in_specs=[pl.BlockSpec(memory_space=plt...  14.3 us
    pad x1, local copies, waits for them, and re-layouts, body(): flat = jnp.pad(cells, ((0, 0), (0, 0), (0, ROW_PAD - cells.shape[-1])))  6.23 us
    pallas_call x1, Pallas kernels, line_spectra(): pl.pallas_call(dft_kernel, out_shape=(out, out), cost_estimate=pl.CostEst...  5.65 us
    scatter x1, local copies, waits for them, and re-layouts, body(): jnp.zeros((total_blocks,), jnp.int32).at[place_at]  3.37 us
    all_to_all x1, local copies, waits for them, and re-layouts, body(): lax.all_to_all(parcel, ('bulk', 'own'), split_axis=0, concat_axis=0, tile...  3.21 us

profile of v5, /device:TPU:1, one launch (start us, length us, event | category | flops | bytes accessed | tf_op | source)
XLA Modules:
  0.0 110.0 jit_solution(644317724777784538)
XLA Ops:
  0.6 0.0 copy-start
  1.3 0.7 fusion.1
  2.1 0.1 reduce_window_sum.11
  2.2 0.8 select_reduce_fusion
  3.1 0.7 fusion.7
  3.7 0.9 scatter_custom_fusion
  4.7 0.0 copy-done
  4.7 1.2 %gather_fusion.1 = s32[96]{0:T(128)S(1)} fusion(s32[96]{0:T(128)S(1)} %bitcast.32, s32[1024]{0:T(1024)S(1)} %pad_clamp_fusion.2), kind=kCustom, calls=%fused_computation.1 | custom fusion | bytes 1152 | tf_op jit(solution)/shard_map/jit(_take)/gather | solution.py:262
  5.9 0.1 reshape.139
  6.0 0.1 copy.28
  6.1 0.7 gather_fusion.2
  6.8 0.1 copy.29
  6.8 0.1 reshape.136
  6.9 0.1 copy.26
  7.0 0.6 reshape.137.src_ref
  7.6 0.7 fusion.6
  8.3 1.2 %gather_fusion = f32[96]{0:T(128)S(1)} fusion(f32[96]{0:T(128)S(1)} %fusion.6, s32[1024]{0:T(1024)S(1)} %pad_clamp_fusion.2), kind=kCustom, calls=%fused_computation | custom fusion | bytes 1152 | tf_op jit(solution)/shard_map/jit(_take)/gather | solution.py:269
  9.5 0.1 reshape.138
  9.6 0.1 copy.27
  9.7 0.1 broadcast_in_dim.103
  9.8 6.2 %pad.4.x_hbm = f32[3,96,6016]{2,1,0:T(8,128)} pad(f32[3,96,5832]{2,1,0:T(8,128)} %bitcast.36, f32[]{:T(128)} %constant.58.clone.1), padding=0_0x0_0x0_184 | pad | bytes 13648900 | tf_op jit(solution)/shard_map/jit(_pad)/pad | solution.py:273
  16.0 0.6 select_bitcast_fusion.code_ref
  16.6 0.7 broadcast_in_dim.104.fac_ref
  17.3 14.3 %shard_map.167 = f32[256,1664]{1,0:T(8,128)} custom-call(s32[96]{0:T(128)} %reshape.137.src_ref, f32[3,96,6016]{2,1,0:T(8,128)} %pad.4.x_hbm, bf16[384,256]{1,0:T(8,128)(2,1)} %constant.113.clone.sel_ref, f32[96,256]{1,0:T(8,128)} %broadcast_in_dim.104.fac_ref, f32[32,128]{1,0:T(8,128)} %select_bitcast_fusion.code_ref), custom_call_target="tpu_custom_call" | custom-call | flops 905969664 | bytes 8634368 | tf_op jit(solution)/shard_map/pallas_call | solution.py:134
  31.6 3.2 %copy.30 = f32[256,1,1664]{2,1,0:T(1,128)S(1)} copy(f32[256,1,1664]{2,0,1:T(8,128)} %bitcast.35) | data formatting | bytes 3407872 | tf_op jit(solution)/shard_map/all_to_all | solution.py:276
  34.8 62.6 %all_to_all.12 = f32[256,1,1664]{2,1,0:T(1,128)S(1)} all-to-all(f32[256,1,1664]{2,1,0:T(1,128)S(1)} %copy.30), channel_id=1, replica_groups=mesh['bulk'=8,'own'=32] {'bulk','own'}, dimensions={0} | all-to-all | bytes 3407872 | tf_op jit(solution)/shard_map/all_to_all | solution.py:276
  97.4 0.1 copy.33
  97.5 0.2 slice.17
  97.7 0.2 select_n.112
  98.0 3.4 %scatter_custom_fusion.1 = s32[384]{0:T(512)S(1)} fusion(s32[768]{0:T(1024)S(1)} %fusion.2, s32[768]{0:T(1024)S(1)} %iota.33, s32[]{:T(128)} %constant.48.clone.1), kind=kCustom, calls=%fused_computation.29 | custom fusion | bytes 1540 | tf_op jit(solution)/shard_map/scatter | solution.py:283
  101.4 0.3 reshape.140
  101.7 1.6 %gather_fusion.3 = f32[384,512]{1,0:T(8,128)S(1)} fusion(f32[768,512]{1,0:T(8,128)S(1)} %reshape.140, s32[1024]{0:T(1024)S(1)} %pad_clamp_fusion), kind=kCustom, calls=%fused_computation.3 | custom fusion | bytes 1574400 | tf_op jit(solution)/shard_map/jit(_take)/gather | solution.py:285
  103.4 1.0 broadcast_select_fusion.x_ref
  104.4 5.6 %shard_map.168 = (f32[32,3072]{1,0:T(8,128)}, f32[32,3072]{1,0:T(8,128)}) custom-call(f32[384,512]{1,0:T(8,128)} %broadcast_select_fusion.x_ref, bf16[384,384]{1,0:T(8,128)(2,1)} %constant.114.clone.c1h, bf16[384,384]{1,0:T(8,128)(2,1)} %constant.115.clone.c1l, bf16[384,384]{1,0:T(8,128)(2,1)} %constant.116.clone.s1h, bf16[384,384]{1,0:T(8,128)(2,1)} %constant.117.clone.s1l, ...), custom_call_target="tpu_custom_call" | custom-call | flops 1207959552 | bytes 3145728 | tf_op jit(solution)/shard_map/pallas_call | solution.py:229
  (15 shorter events, 0.1 us)
Async XLA Ops:
  0.6 4.0 %copy-start = (s32[1,1,96]{2,1,0:T(1,128)S(1)}, s32[1,1,96]{2,1,0:T(1,128)}, u32[]{:S(2)}) copy-start(s32[1,1,96]{2,1,0:T(1,128)} %param.18) | copy-start | bytes 1156

commit v6 on v4

--- a/solution.py
+++ b/solution.py
@@ -79,64 +79,57 @@
     return w[:, :PLANE_PAD]
 
 
-def divergence_kernel(x_ref, sel_ref, p_ref, code_ref, o_ref):
-    h = pl.program_id(0)
+def divergence_kernel(src_ref, x_hbm, sel_ref, fac_ref, code_ref, o_ref, buf, sem):
+    owners = src_ref.shape[0]
+    chunk_rows = o_ref.shape[0]
+    groups = chunk_rows // owners
+    planes_per_group = BOX // groups
+    for r in range(owners):
+        pltpu.make_async_copy(
+            x_hbm.at[:, pl.ds(src_ref[r], 1), :], buf.at[:, pl.ds(r, 1), :], sem.at[0]
+        ).start()
+    data_w = o_ref.shape[1] - code_ref.shape[1]
+    for g in range(groups):
+        o_ref[g * owners:(g + 1) * owners, data_w:] = code_ref[...]
+    sel = sel_ref[...]
+    pltpu.make_async_copy(x_hbm.at[:, pl.ds(0, owners), :], buf, sem.at[0]).wait()
     pieces = []
     for i in range(BOX):
-        u = _plane(x_ref, 0, i + 1)
-        w = _plane(x_ref, 2, i + 1)
+        u = _plane(buf, 0, i + 1)
+        w = _plane(buf, 2, i + 1)
         along_x = pltpu.roll(u, PLANE_PAD - 1, 1) - pltpu.roll(u, 1, 1)
-        along_y = _plane(x_ref, 1, i + 2) - _plane(x_ref, 1, i)
+        along_y = _plane(buf, 1, i + 2) - _plane(buf, 1, i)
         along_z = pltpu.roll(w, PLANE_PAD - GHOST, 1) - pltpu.roll(w, GHOST, 1)
         pieces.append(along_x + (along_y + along_z))
-    interior = _exact_right(jnp.concatenate(pieces, axis=0), sel_ref[...])
-    rows = p_ref.shape[2]
-    permute = p_ref[0]
-    chunk_rows = o_ref.shape[0]
-    data_w = o_ref.shape[1] - code_ref.shape[1]
-    owners = code_ref.shape[0]
-    per_pair = permute.shape[0] // owners
-    groups = chunk_rows // owners
-    planes_per_group = BOX // groups
-    piece_w = data_w // per_pair
-
-    @pl.when(h == 0)
-    def _():
-        o_ref[...] = jnp.zeros_like(o_ref)
-        for g in range(groups):
-            o_ref[g * owners:(g + 1) * owners, data_w:] = code_ref[...]
-
+    interior = _exact_right(jnp.concatenate(pieces, axis=0), sel)
+    fac = fac_ref[...]
     for i in range(BOX):
-        moved = _exact_left(permute, interior[i * rows:(i + 1) * rows])
         g, half = divmod(i, planes_per_group)
-        for t in range(per_pair):
-            lane0 = t * piece_w + half * FACE
-            o_ref[g * owners:(g + 1) * owners, lane0:lane0 + FACE] += moved[t * owners:(t + 1) * owners]
-
-
-def source_divergence(flat, permute, codes, groups, halves=2):
-    slots = flat.shape[1]
-    part = slots // halves
-    owners = codes.shape[0]
-    out_w = BOX * FACE // groups * (slots // owners) + CODE_W
+        o_ref[g * owners:(g + 1) * owners, half * FACE:(half + 1) * FACE] = interior[i * owners:(i + 1) * owners] * fac
+
+
+def source_divergence(flat, source, factor, codes, groups):
+    owners = source.shape[0]
+    out_w = BOX * FACE // groups + CODE_W
     sel = selection_table()
+    vmem = pl.BlockSpec(memory_space=pltpu.VMEM)
+    operands = [source, flat, sel, jnp.broadcast_to(factor[:, None], (owners, FACE)), codes]
     return pl.pallas_call(
         divergence_kernel,
-        grid=(halves,),
-        in_specs=[
-            pl.BlockSpec((3, part, ROW_PAD), lambda h: (0, h, 0)),
-            pl.BlockSpec((PLANE_PAD, FACE), lambda h: (0, 0)),
-            pl.BlockSpec((1, slots, part), lambda h: (h, 0, 0)),
-            pl.BlockSpec((owners, CODE_W), lambda h: (0, 0)),
+        in_specs=[pl.BlockSpec(memory_space=pltpu.SMEM), pl.BlockSpec(memory_space=pl.ANY)]
+        + [vmem] * (len(operands) - 2),
+        out_specs=vmem,
+        out_shape=jax.ShapeDtypeStruct((groups * owners, out_w), F32),
+        scratch_shapes=[
+            pltpu.VMEM((3, owners, flat.shape[2]), F32),
+            pltpu.SemaphoreType.DMA((1,)),
         ],
-        out_specs=pl.BlockSpec((groups * owners, out_w), lambda h: (0, 0)),
-        out_shape=jax.ShapeDtypeStruct((groups * owners, out_w), F32),
         cost_estimate=pl.CostEstimate(
-            flops=2 * slots * BOX * PLANE_PAD * FACE * 3 + 2 * slots * slots * BOX * FACE * 3,
-            bytes_accessed=4 * (3 * slots * ROW_PAD + groups * owners * out_w),
+            flops=2 * owners * BOX * PLANE_PAD * FACE * 3,
+            bytes_accessed=4 * (3 * owners * ROW_PAD + groups * owners * out_w),
             transcendentals=0,
         ),
-    )(flat, sel, jnp.transpose(permute.reshape(slots, halves, part), (1, 0, 2)), codes)
+    )(*operands)
 
 
 def _split_np(t):
@@ -241,8 +234,6 @@
     position = jnp.where(filled, destination * per_pair + order_rank, parcel_rows)
     parcel_ids = jnp.arange(parcel_rows, dtype=jnp.int32)
     factor = level_factor(box_level[0, 0])
-    row_of = jnp.where(filled, order_rank * owners + destination, parcel_rows)
-    permute = jnp.where(row_of[None, :] == parcel_ids[:, None], factor[None, :], 0.0).astype(BF16)
     source = jnp.full((parcel_rows,), slot_total, jnp.int32).at[position].set(slot_ids, mode="drop")
     occupied = source < slot_total
     source_safe = jnp.minimum(source, slot_total - 1)
@@ -253,21 +244,28 @@
         jnp.take(blocks_out.reshape(owners, per_pair), jnp.minimum(code_lanes, per_pair - 1), axis=1),
         0.0,
     )
+    row_factor = jnp.where(occupied, jnp.take(factor, source_safe), 0.0)
 
     cells = velocity[:, 0, 0]
     flat = jnp.pad(cells, ((0, 0), (0, 0), (0, ROW_PAD - cells.shape[-1])))
-    parcel = source_divergence(flat, permute, codes, groups)
-
-    arrived = lax.all_to_all(parcel, ("bulk", "own"), split_axis=0, concat_axis=0, tiled=True)
+    by_rank = lambda v: v.reshape(owners, per_pair).T
+    sources = by_rank(source_safe)
+    factors = by_rank(row_factor)
+    arrived = []
+    for t in range(per_pair):
+        parcel = source_divergence(flat, sources[t], factors[t], codes, groups)
+        if t:
+            parcel = parcel[:, :BOX * FACE // groups]
+        arrived.append(lax.all_to_all(parcel, ("bulk", "own"), split_axis=0, concat_axis=0, tiled=True))
     piece_w = BOX * FACE // groups
-    data_w = piece_w * per_pair
-    code_in = arrived[:, data_w:data_w + per_pair].reshape(-1)
+    code_in = arrived[0][:, piece_w:piece_w + per_pair].T.reshape(-1)
     total_blocks = groups * held_blocks
     place_at = jnp.where(code_in >= 0, code_in.astype(jnp.int32), total_blocks)
     arrived_ids = jnp.arange(code_in.shape[0], dtype=jnp.int32)
     chosen = jnp.zeros((total_blocks,), jnp.int32).at[place_at].set(arrived_ids, mode="drop")
-    pieces = arrived[:, :data_w].reshape(-1, piece_w)
-    cosine, sine_vals = line_spectra(jnp.take(pieces, chosen, axis=0))
+    pieces = jnp.concatenate([arrived[0][:, :piece_w]] + arrived[1:], axis=0)
+    x = jnp.take(pieces, chosen, axis=0)
+    cosine, sine_vals = line_spectra(x)
     return (cosine[None], sine_vals[None])
 
 

time: 109 us -> 134 us (1.23)
  blocking collectives: 61.6 us -> 0 us
  waiting for transfers between devices: 0 us -> 43.2 us
  starting transfers between devices: 0 us -> 25.8 us
  Pallas kernels: 19.4 us -> 31.6 us
  local copies, waits for them, and re-layouts: 19.2 us -> 26.4 us
  other arithmetic: 6.74 us -> 4.9 us
    all_to_all x1 -> x0, blocking collectives: 61.6 us -> none  [body(): lax.all_to_all(parcel, ('bulk', 'own'), split_axis=0, concat_axis=0, tile...]
    all_to_all x0 -> x3, waiting for transfers between devices: none -> 43.2 us  [body(): lax.all_to_all(parcel, ('bulk', 'own'), split_axis=0, concat_axis=0, tile...]
    all_to_all x0 -> x3, starting transfers between devices: none -> 25.8 us  [body(): lax.all_to_all(parcel, ('bulk', 'own'), split_axis=0, concat_axis=0, tile...]
    pallas_call x1 -> x3, Pallas kernels: 13.8 us -> 25.9 us  [source_divergence(): pl.pallas_call(divergence_kernel, in_specs=[pl.BlockSpec(memory_space=plt...]
    all_to_all x1 -> x5, local copies, waits for them, and re-layouts: 3.21 us -> 7.46 us  [body(): lax.all_to_all(parcel, ('bulk', 'own'), split_axis=0, concat_axis=0, tile...]
    broadcast_in_dim x0 -> x3, local copies, waits for them, and re-layouts: none -> 2.06 us  [source_divergence(): jnp.broadcast_to(factor[:, None], (owners, FACE))]
    gather x1 -> x2, local copies, waits for them, and re-layouts: 1.62 us -> 2.85 us  [the longest x1 1.62 us: body(): x = jnp.take(pieces, chosen, axis=0)]
  transfers between devices with their start and end apart: 0 -> 3, of which waited for: 0 -> 3; matrix products, arithmetic and copies ran while one was open for 0% -> 5% of each run, Pallas kernels for 0% -> 13%
where the time goes in v6:
time: 134 us; the launch traced here: 133 us
  waiting for transfers between devices  43.2 us (32%)
  Pallas kernels  31.6 us (24%)
  local copies, waits for them, and re-layouts  26.4 us (20%)
  starting transfers between devices  25.8 us (19%)
  other arithmetic  4.9 us (4%)
  between operations  1.57 us (1%)
    all_to_all x3, waiting for transfers between devices, body(): lax.all_to_all(parcel, ('bulk', 'own'), split_axis=0, concat_axis=0, tile...  43.2 us
    pallas_call x3, Pallas kernels, source_divergence(): pl.pallas_call(divergence_kernel, in_specs=[pl.BlockSpec(memory_space=plt...  25.9 us
    all_to_all x3, starting transfers between devices, body(): lax.all_to_all(parcel, ('bulk', 'own'), split_axis=0, concat_axis=0, tile...  25.8 us
    all_to_all x5, local copies, waits for them, and re-layouts, body(): lax.all_to_all(parcel, ('bulk', 'own'), split_axis=0, concat_axis=0, tile...  7.46 us
    pad x1, local copies, waits for them, and re-layouts, body(): flat = jnp.pad(cells, ((0, 0), (0, 0), (0, ROW_PAD - cells.shape[-1])))  6.24 us
    pallas_call x1, Pallas kernels, line_spectra(): pl.pallas_call(dft_kernel, out_shape=(out, out), cost_estimate=pl.CostEst...  5.65 us
    scatter x1, local copies, waits for them, and re-layouts, body(): jnp.zeros((total_blocks,), jnp.int32).at[place_at]  3.37 us
  transfers between devices with their start and end apart: 3, of which 3 were waited for; matrix products, arithmetic and copies ran while one was open for 5% of the time, Pallas kernels for 13%

profile of v6, /device:TPU:1, one launch (start us, length us, event | category | flops | bytes accessed | tf_op | source)
XLA Modules:
  0.0 133.4 jit_solution(8655453201760713430)
XLA Ops:
  0.6 0.0 copy-start
  1.3 0.7 fusion.1
  2.1 0.1 reduce_window_sum.11
  2.2 0.8 select_reduce_fusion
  3.1 0.7 fusion.7
  3.7 0.9 scatter_custom_fusion
  4.7 0.0 copy-done
  4.7 1.2 gather_fusion.1
  5.9 0.1 reshape.136
  6.0 0.8 slice_reduce_fusion.5
  6.8 0.7 fusion.6
  7.4 1.2 gather_fusion
  8.7 0.1 reshape.137
  8.8 0.2 slice_reduce_fusion.4
  9.0 0.1 reshape.138
  9.1 0.1 copy.25
  9.2 0.7 gather_fusion.2
  9.8 0.1 copy.26
  9.9 6.2 %pad.4.x_hbm = f32[3,96,6016]{2,1,0:T(8,128)} pad(f32[3,96,5832]{2,1,0:T(8,128)} %bitcast.49, f32[]{:T(128)} %constant.58.clone.1), padding=0_0x0_0x0_184 | pad | bytes 13648900 | tf_op jit(solution)/shard_map/jit(_pad)/pad | solution.py:250
  16.1 0.6 select_bitcast_fusion.1.code_ref
  16.7 0.7 broadcast_in_dim.131.fac_ref
  17.4 8.6 %shard_map.187 = f32[256,640]{1,0:T(8,128)} custom-call(s32[32]{0:T(128)} %get-tuple-element.10.src_ref, f32[3,96,6016]{2,1,0:T(8,128)} %pad.4.x_hbm, bf16[384,256]{1,0:T(8,128)(2,1)} %constant.113.clone.sel_ref, f32[32,256]{1,0:T(8,128)} %broadcast_in_dim.131.fac_ref, f32[32,128]{1,0:T(8,128)} %select_bitcast_fusion.1.code_ref), custom_call_target="tpu_custom_call" | custom-call | flops 301989888 | bytes 2965504 | tf_op jit(solution)/shard_map/pallas_call | solution.py:117
  26.1 1.1 slice_bitcast_fusion
  27.1 1.4 %copy.30 = f32[256,1,512]{2,1,0:T(1,128)} copy(f32[256,1,512]{2,0,1:T(8,128)S(1)} %slice_bitcast_fusion) | data formatting | bytes 1048576 | tf_op jit(solution)/shard_map/all_to_all | solution.py:259
  28.5 15.0 %all-to-all-start.2 = ((f32[256,1,512]{2,1,0:T(1,128)}), f32[256,1,512]{2,1,0:T(1,128)S(1)}, u32[]{:S(2)}, u32[]{:S(2)}) async-start(f32[256,1,512]{2,1,0:T(1,128)} %copy.30), calls=%async_computation.2 | async-start | bytes 1048576 | tf_op jit(solution)/shard_map/all_to_all | solution.py:259
  43.5 0.7 broadcast_in_dim.129.fac_ref
  44.2 8.6 %shard_map.186 = f32[256,640]{1,0:T(8,128)} custom-call(s32[32]{0:T(128)} %get-tuple-element.11.src_ref, f32[3,96,6016]{2,1,0:T(8,128)} %pad.4.x_hbm, bf16[384,256]{1,0:T(8,128)(2,1)} %constant.113.clone.sel_ref, f32[32,256]{1,0:T(8,128)} %broadcast_in_dim.129.fac_ref, f32[32,128]{1,0:T(8,128)} %select_bitcast_fusion.1.code_ref), custom_call_target="tpu_custom_call" | custom-call | flops 301989888 | bytes 2965504 | tf_op jit(solution)/shard_map/pallas_call | solution.py:117
  52.8 1.1 slice_bitcast_fusion.1
  53.9 1.3 %copy.29 = f32[256,1,512]{2,1,0:T(1,128)} copy(f32[256,1,512]{2,0,1:T(8,128)S(1)} %slice_bitcast_fusion.1) | data formatting | bytes 1048576 | tf_op jit(solution)/shard_map/all_to_all | solution.py:259
  55.2 9.6 %all-to-all-done.2 = f32[256,1,512]{2,1,0:T(1,128)S(1)} async-done(((f32[256,1,512]{2,1,0:T(1,128)}), f32[256,1,512]{2,1,0:T(1,128)S(1)}, u32[]{:S(2)}, u32[]{:S(2)}) %all-to-all-start.2) | async-done | bytes 524320 | tf_op jit(solution)/shard_map/all_to_all | solution.py:259
  64.9 5.4 %all-to-all-start.1 = ((f32[256,1,512]{2,1,0:T(1,128)}), f32[256,1,512]{2,1,0:T(1,128)S(1)}, u32[]{:S(2)}, u32[]{:S(2)}) async-start(f32[256,1,512]{2,1,0:T(1,128)} %copy.29), calls=%async_computation.1 | async-start | bytes 1048576 | tf_op jit(solution)/shard_map/all_to_all | solution.py:259
  70.3 0.7 broadcast_in_dim.118.fac_ref
  71.0 8.6 %shard_map.185 = f32[256,640]{1,0:T(8,128)} custom-call(s32[32]{0:T(128)} %get-tuple-element.9.src_ref, f32[3,96,6016]{2,1,0:T(8,128)} %pad.4.x_hbm, bf16[384,256]{1,0:T(8,128)(2,1)} %constant.113.clone.sel_ref, f32[32,256]{1,0:T(8,128)} %broadcast_in_dim.118.fac_ref, f32[32,128]{1,0:T(8,128)} %select_bitcast_fusion.1.code_ref), custom_call_target="tpu_custom_call" | custom-call | flops 301989888 | bytes 2965504 | tf_op jit(solution)/shard_map/pallas_call | solution.py:117
  79.6 2.6 %copy.27 = f32[256,1,640]{2,1,0:T(1,128)} copy(f32[256,1,640]{2,0,1:T(8,128)} %bitcast.52) | data formatting | bytes 1310720 | tf_op jit(solution)/shard_map/all_to_all | solution.py:259
  82.2 9.6 %all-to-all-done.1 = f32[256,1,512]{2,1,0:T(1,128)S(1)} async-done(((f32[256,1,512]{2,1,0:T(1,128)}), f32[256,1,512]{2,1,0:T(1,128)S(1)}, u32[]{:S(2)}, u32[]{:S(2)}) %all-to-all-start.1) | async-done | bytes 524320 | tf_op jit(solution)/shard_map/all_to_all | solution.py:259
  91.8 5.4 %all-to-all-start = ((f32[256,1,640]{2,1,0:T(1,128)}), f32[256,1,640]{2,1,0:T(1,128)S(1)}, u32[]{:S(2)}, u32[]{:S(2)}) async-start(f32[256,1,640]{2,1,0:T(1,128)} %copy.27), calls=%async_computation | async-start | bytes 1310720 | tf_op jit(solution)/shard_map/all_to_all | solution.py:259
  97.3 24.0 %all-to-all-done = f32[256,1,640]{2,1,0:T(1,128)S(1)} async-done(((f32[256,1,640]{2,1,0:T(1,128)}), f32[256,1,640]{2,1,0:T(1,128)S(1)}, u32[]{:S(2)}, u32[]{:S(2)}) %all-to-all-start) | async-done | bytes 655392 | tf_op jit(solution)/shard_map/all_to_all | solution.py:259
  121.4 0.1 slice.51
  121.5 0.1 copy.28
  121.6 3.4 %scatter_custom_fusion.1 = s32[384]{0:T(512)S(1)} fusion(s32[768]{0:T(1024)S(1)} %fusion.2, s32[768]{0:T(1024)S(1)} %iota.33, s32[]{:T(128)} %constant.48.clone.1), kind=kCustom, calls=%fused_computation.40 | custom fusion | bytes 1540 | tf_op jit(solution)/shard_map/scatter | solution.py:265
  125.0 0.1 pad_maximum_fusion
  125.2 1.6 %gather_fusion.3 = f32[384,512]{1,0:T(8,128)S(1)} fusion(f32[768,512]{1,0:T(8,128)S(1)} %pad_maximum_fusion, s32[1024]{0:T(1024)S(1)} %pad_clamp_fusion), kind=kCustom, calls=%fused_computation.3 | custom fusion | bytes 1574400 | tf_op jit(solution)/shard_map/jit(_take)/gather | solution.py:267
  126.8 1.0 broadcast_select_fusion.x_ref
  127.8 5.6 %shard_map.188 = (f32[32,3072]{1,0:T(8,128)}, f32[32,3072]{1,0:T(8,128)}) custom-call(f32[384,512]{1,0:T(8,128)} %broadcast_select_fusion.x_ref, bf16[384,384]{1,0:T(8,128)(2,1)} %constant.114.clone.c1h, bf16[384,384]{1,0:T(8,128)(2,1)} %constant.115.clone.c1l, bf16[384,384]{1,0:T(8,128)(2,1)} %constant.116.clone.s1h, bf16[384,384]{1,0:T(8,128)(2,1)} %constant.117.clone.s1l, ...), custom_call_target="tpu_custom_call" | custom-call | flops 1207959552 | bytes 3145728 | tf_op jit(solution)/shard_map/pallas_call | solution.py:207
  (19 shorter events, 0.2 us)
Async XLA Ops:
  0.6 4.0 %copy-start = (s32[1,1,96]{2,1,0:T(1,128)S(1)}, s32[1,1,96]{2,1,0:T(1,128)}, u32[]{:S(2)}) copy-start(s32[1,1,96]{2,1,0:T(1,128)} %param.20) | copy-start | bytes 1156
  28.5 36.4 %all-to-all-start.2 = ((f32[256,1,512]{2,1,0:T(1,128)}), f32[256,1,512]{2,1,0:T(1,128)S(1)}, u32[]{:S(2)}, u32[]{:S(2)}) async-start(f32[256,1,512]{2,1,0:T(1,128)} %copy.30), calls=%async_computation.2 | async-start | bytes 1048576 | tf_op jit(solution)/shard_map/all_to_all | solution.py:259
  64.9 26.9 %all-to-all-start.1 = ((f32[256,1,512]{2,1,0:T(1,128)}), f32[256,1,512]{2,1,0:T(1,128)S(1)}, u32[]{:S(2)}, u32[]{:S(2)}) async-start(f32[256,1,512]{2,1,0:T(1,128)} %copy.29), calls=%async_computation.1 | async-start | bytes 1048576 | tf_op jit(solution)/shard_map/all_to_all | solution.py:259
  91.8 29.5 %all-to-all-start = ((f32[256,1,640]{2,1,0:T(1,128)}), f32[256,1,640]{2,1,0:T(1,128)S(1)}, u32[]{:S(2)}, u32[]{:S(2)}) async-start(f32[256,1,640]{2,1,0:T(1,128)} %copy.27), calls=%async_computation | async-start | bytes 1310720 | tf_op jit(solution)/shard_map/all_to_all | solution.py:259

commit v7 on v5

--- a/solution.py
+++ b/solution.py
@@ -248,30 +248,26 @@
     slot_ids = jnp.arange(slot_total, dtype=jnp.int32)
     destination = new_owner[0, 0]
     filled = slot_ids < box_count[0, 0]
-    owner_hits = (
-        filled[:, None] & (destination[:, None] == jnp.arange(owners, dtype=jnp.int32)[None, :])
-    ).astype(jnp.int32)
-    earlier = jnp.cumsum(owner_hits, axis=0) - owner_hits
-    order_rank = jnp.sum(earlier * owner_hits, axis=1)
-    position = jnp.where(filled, destination * per_pair + order_rank, parcel_rows)
+    same_owner = filled[:, None] & filled[None, :] & (destination[:, None] == destination[None, :])
+    order_rank = jnp.sum((same_owner & (slot_ids[None, :] < slot_ids[:, None])).astype(jnp.int32), axis=1)
+    row_of = jnp.where(filled, order_rank * owners + destination, parcel_rows)
     parcel_ids = jnp.arange(parcel_rows, dtype=jnp.int32)
+    match = row_of[None, :] == parcel_ids[:, None]
     factor = level_factor(box_level[0, 0])
-    source = jnp.full((parcel_rows,), slot_total, jnp.int32).at[position].set(slot_ids, mode="drop")
-    occupied = source < slot_total
-    source_safe = jnp.minimum(source, slot_total - 1)
-    blocks_out = jnp.where(occupied, jnp.take(box_block[0, 0], source_safe), -1).astype(F32)
+    source_safe = jnp.sum(jnp.where(match, slot_ids[None, :], 0), axis=1)
+    row_factor = jnp.sum(jnp.where(match, factor[None, :], 0.0), axis=1)
+    row_block = jnp.sum(jnp.where(match, box_block[0, 0][None, :] + 1, 0), axis=1) - 1
     code_lanes = jnp.arange(CODE_W, dtype=jnp.int32)
+    by_owner = row_block.reshape(per_pair, owners).T
     codes = jnp.where(
         code_lanes[None, :] < per_pair,
-        jnp.take(blocks_out.reshape(owners, per_pair), jnp.minimum(code_lanes, per_pair - 1), axis=1),
-        0.0,
-    )
-    row_factor = jnp.where(occupied, jnp.take(factor, source_safe), 0.0)
-    by_rank = lambda v: v.reshape(owners, per_pair).T.reshape(-1)
+        jnp.take(by_owner, jnp.minimum(code_lanes, per_pair - 1), axis=1),
+        -1,
+    ).astype(F32)
 
     cells = velocity[:, 0, 0]
     flat = jnp.pad(cells, ((0, 0), (0, 0), (0, ROW_PAD - cells.shape[-1])))
-    parcel = source_divergence(flat, by_rank(source_safe), by_rank(row_factor), codes, groups)
+    parcel = source_divergence(flat, source_safe, row_factor, codes, groups)
 
     arrived = lax.all_to_all(parcel, ("bulk", "own"), split_axis=0, concat_axis=0, tiled=True)
     piece_w = BOX * FACE // groups
@@ -280,7 +276,8 @@
     total_blocks = groups * held_blocks
     place_at = jnp.where(code_in >= 0, code_in.astype(jnp.int32), total_blocks)
     arrived_ids = jnp.arange(code_in.shape[0], dtype=jnp.int32)
-    chosen = jnp.zeros((total_blocks,), jnp.int32).at[place_at].set(arrived_ids, mode="drop")
+    block_ids = jnp.arange(total_blocks, dtype=jnp.int32)
+    chosen = jnp.sum(jnp.where(place_at[None, :] == block_ids[:, None], arrived_ids[None, :], 0), axis=1)
     pieces = arrived[:, :data_w].reshape(-1, piece_w)
     cosine, sine_vals = line_spectra(jnp.take(pieces, chosen, axis=0))
     return (cosine[None], sine_vals[None])

time: 110 us -> 103 us (0.936)
  local copies, waits for them, and re-layouts: 21.3 us -> 13.4 us
  Pallas kernels: 19.9 us -> 17.7 us
  blocking collectives: 62.6 us -> 64.4 us
    scatter x2 -> x0, local copies, waits for them, and re-layouts: 4.24 us -> none  [the longest x1 3.37 us: body(): jnp.zeros((total_blocks,), jnp.int32).at[place_at]]
    gather x4 -> x2, local copies, waits for them, and re-layouts: 3.16 us -> 0.7 us  [body(): jnp.take(by_owner, jnp.minimum(code_lanes, per_pair - 1), axis=1)]
    pallas_call x1, Pallas kernels: 14.3 us -> 12.1 us  [source_divergence(): pl.pallas_call(divergence_kernel, in_specs=[pl.BlockSpec(memory_space=plt...]
    all_to_all x1, blocking collectives: 62.6 us -> 64.4 us  [body(): lax.all_to_all(parcel, ('bulk', 'own'), split_axis=0, concat_axis=0, tile...]
where the time goes in v7:
time: 103 us; the launch traced here: 102 us
  blocking collectives  64.4 us (63%)
  Pallas kernels  17.7 us (17%)
  local copies, waits for them, and re-layouts  13.4 us (13%)
  other arithmetic  5.54 us (5%)
  between operations  1.37 us (1%)
    all_to_all x1, blocking collectives, body(): lax.all_to_all(parcel, ('bulk', 'own'), split_axis=0, concat_axis=0, tile...  64.4 us
    pallas_call x1, Pallas kernels, source_divergence(): pl.pallas_call(divergence_kernel, in_specs=[pl.BlockSpec(memory_space=plt...  12.1 us
    pad x1, local copies, waits for them, and re-layouts, body(): flat = jnp.pad(cells, ((0, 0), (0, 0), (0, ROW_PAD - cells.shape[-1])))  6.24 us
    pallas_call x1, Pallas kernels, line_spectra(): pl.pallas_call(dft_kernel, out_shape=(out, out), cost_estimate=pl.CostEst...  5.64 us
    all_to_all x1, local copies, waits for them, and re-layouts, body(): lax.all_to_all(parcel, ('bulk', 'own'), split_axis=0, concat_axis=0, tile...  3.21 us

profile of v7, /device:TPU:1, one launch (start us, length us, event | category | flops | bytes accessed | tf_op | source)
XLA Modules:
  0.0 102.4 jit_solution(10339589195823425236)
XLA Ops:
  1.3 0.7 add_bitcast_fusion
  2.0 0.7 fusion.2
  2.6 0.9 convert_reduce_fusion
  3.6 0.7 add_select_fusion
  4.2 0.1 select_reduce_fusion.2
  4.3 0.6 select_reduce_fusion.1
  5.0 0.1 sub.6
  5.1 0.6 gather_fusion
  5.7 0.1 copy.22
  5.8 6.2 %pad.4.x_hbm = f32[3,96,6016]{2,1,0:T(8,128)} pad(f32[3,96,5832]{2,1,0:T(8,128)} %bitcast.25, f32[]{:T(128)} %constant.30.clone.1), padding=0_0x0_0x0_184 | pad | bytes 13648900 | tf_op jit(solution)/shard_map/jit(_pad)/pad | solution.py:269
  12.0 0.6 convert_bitcast_fusion.code_ref
  12.6 0.7 broadcast_in_dim.123.fac_ref
  13.3 12.1 %shard_map.167 = f32[256,1664]{1,0:T(8,128)} custom-call(s32[96]{0:T(128)} %get-tuple-element.7.src_ref, f32[3,96,6016]{2,1,0:T(8,128)} %pad.4.x_hbm, bf16[384,256]{1,0:T(8,128)(2,1)} %constant.81.clone.sel_ref, f32[96,256]{1,0:T(8,128)} %broadcast_in_dim.123.fac_ref, f32[32,128]{1,0:T(8,128)} %convert_bitcast_fusion.code_ref), custom_call_target="tpu_custom_call" | custom-call | flops 905969664 | bytes 8634368 | tf_op jit(solution)/shard_map/pallas_call | solution.py:134
  25.4 3.2 %copy.23 = f32[256,1,1664]{2,1,0:T(1,128)S(1)} copy(f32[256,1,1664]{2,0,1:T(8,128)} %bitcast.24) | data formatting | bytes 3407872 | tf_op jit(solution)/shard_map/all_to_all | solution.py:272
  28.6 64.4 %all_to_all.12 = f32[256,1,1664]{2,1,0:T(1,128)S(1)} all-to-all(f32[256,1,1664]{2,1,0:T(1,128)S(1)} %copy.23), channel_id=1, replica_groups=mesh['bulk'=8,'own'=32] {'bulk','own'}, dimensions={0} | all-to-all | bytes 3407872 | tf_op jit(solution)/shard_map/all_to_all | solution.py:272
  93.0 0.1 copy.26
  93.2 0.2 slice.13
  93.4 0.2 select_n.95
  93.6 0.2 select_reduce_fusion
  93.8 0.3 reshape.115
  94.2 1.6 %gather_fusion.1 = f32[384,512]{1,0:T(8,128)S(1)} fusion(f32[768,512]{1,0:T(8,128)S(1)} %reshape.115, s32[1024]{0:T(1024)S(1)} %pad_clamp_fusion), kind=kCustom, calls=%fused_computation.1 | custom fusion | bytes 1574400 | tf_op jit(solution)/shard_map/jit(_take)/gather | solution.py:282
  95.8 1.0 broadcast_select_fusion.x_ref
  96.8 5.6 %shard_map.168 = (f32[32,3072]{1,0:T(8,128)}, f32[32,3072]{1,0:T(8,128)}) custom-call(f32[384,512]{1,0:T(8,128)} %broadcast_select_fusion.x_ref, bf16[384,384]{1,0:T(8,128)(2,1)} %constant.82.clone.c1h, bf16[384,384]{1,0:T(8,128)(2,1)} %constant.83.clone.c1l, bf16[384,384]{1,0:T(8,128)(2,1)} %constant.84.clone.s1h, bf16[384,384]{1,0:T(8,128)(2,1)} %constant.85.clone.s1l, ...), custom_call_target="tpu_custom_call" | custom-call | flops 1207959552 | bytes 3145728 | tf_op jit(solution)/shard_map/pallas_call | solution.py:229
  (9 shorter events, 0.1 us)

commit v8 on v7

--- a/solution.py
+++ b/solution.py
@@ -79,7 +79,7 @@
     return w[:, :PLANE_PAD]
 
 
-def divergence_kernel(src_ref, x_hbm, sel_ref, fac_ref, code_ref, o_ref, buf, sem):
+def divergence_kernel(src_ref, x_hbm, v_hbm, sel_ref, fac_ref, code_ref, o_ref, buf_uw, buf_v, sem):
     owners = code_ref.shape[0]
     per_pair = src_ref.shape[0] // owners
     chunk_rows = o_ref.shape[0]
@@ -90,14 +90,18 @@
 
     def fetch(t, slot):
         for r in range(owners):
+            row = src_ref[t * owners + r]
+            for k, field in enumerate((0, 2)):
+                pltpu.make_async_copy(
+                    x_hbm.at[field, pl.ds(row, 1), :], buf_uw.at[slot, k, pl.ds(r, 1), :], sem.at[slot, 0]
+                ).start()
             pltpu.make_async_copy(
-                x_hbm.at[:, pl.ds(src_ref[t * owners + r], 1), :],
-                buf.at[slot, :, pl.ds(r, 1), :],
-                sem.at[slot],
+                v_hbm.at[pl.ds(row, 1), :], buf_v.at[slot, 0, pl.ds(r, 1), :], sem.at[slot, 1]
             ).start()
 
     def wait(slot):
-        pltpu.make_async_copy(x_hbm.at[:, pl.ds(0, owners), :], buf.at[slot], sem.at[slot]).wait()
+        pltpu.make_async_copy(x_hbm.at[pl.ds(0, 2), pl.ds(0, owners), :], buf_uw.at[slot], sem.at[slot, 0]).wait()
+        pltpu.make_async_copy(v_hbm.at[pl.ds(0, owners), :], buf_v.at[slot, 0], sem.at[slot, 1]).wait()
 
     fetch(0, 0)
     for g in range(groups):
@@ -108,13 +112,15 @@
         if t + 1 < per_pair:
             fetch(t + 1, 1 - slot)
         wait(slot)
-        x_ref = buf.at[slot]
+        uw_ref = buf_uw.at[slot]
+        v_ref = buf_v.at[slot]
+        v_planes = [_plane(v_ref, 0, p) for p in range(GHOST)]
         pieces = []
         for i in range(BOX):
-            u = _plane(x_ref, 0, i + 1)
-            w = _plane(x_ref, 2, i + 1)
+            u = _plane(uw_ref, 0, i + 1)
+            w = _plane(uw_ref, 1, i + 1)
             along_x = pltpu.roll(u, PLANE_PAD - 1, 1) - pltpu.roll(u, 1, 1)
-            along_y = _plane(x_ref, 1, i + 2) - _plane(x_ref, 1, i)
+            along_y = v_planes[i + 2] - v_planes[i]
             along_z = pltpu.roll(w, PLANE_PAD - GHOST, 1) - pltpu.roll(w, GHOST, 1)
             pieces.append(along_x + (along_y + along_z))
         interior = _exact_right(jnp.concatenate(pieces, axis=0), sel)
@@ -125,16 +131,18 @@
             o_ref[g * owners:(g + 1) * owners, lane0:lane0 + FACE] = interior[i * owners:(i + 1) * owners] * fac
 
 
-def source_divergence(flat, source, factor, codes, groups):
-    slots = flat.shape[1]
+def source_divergence(cells, source, factor, codes, groups):
+    slots = cells.shape[1]
     owners = codes.shape[0]
     out_w = BOX * FACE // groups * (slots // owners) + CODE_W
     sel = selection_table()
+    spanwise = jnp.pad(cells[1], ((0, 0), (0, ROW_PAD - cells.shape[-1])))
     vmem = pl.BlockSpec(memory_space=pltpu.VMEM)
     return pl.pallas_call(
         divergence_kernel,
         in_specs=[
             pl.BlockSpec(memory_space=pltpu.SMEM),
+            pl.BlockSpec(memory_space=pl.ANY),
             pl.BlockSpec(memory_space=pl.ANY),
             vmem,
             vmem,
@@ -143,15 +151,16 @@
         out_specs=vmem,
         out_shape=jax.ShapeDtypeStruct((groups * owners, out_w), F32),
         scratch_shapes=[
-            pltpu.VMEM((2, 3, owners, flat.shape[2]), F32),
-            pltpu.SemaphoreType.DMA((2,)),
+            pltpu.VMEM((2, 2, owners, cells.shape[2]), F32),
+            pltpu.VMEM((2, 1, owners, ROW_PAD), F32),
+            pltpu.SemaphoreType.DMA((2, 2)),
         ],
         cost_estimate=pl.CostEstimate(
             flops=2 * slots * BOX * PLANE_PAD * FACE * 3,
             bytes_accessed=4 * (3 * slots * ROW_PAD + groups * owners * out_w),
             transcendentals=0,
         ),
-    )(source, flat, sel, jnp.broadcast_to(factor[:, None], (slots, FACE)), codes)
+    )(source, cells, spanwise, sel, jnp.broadcast_to(factor[:, None], (slots, FACE)), codes)
 
 
 def _split_np(t):
@@ -265,9 +274,7 @@
         -1,
     ).astype(F32)
 
-    cells = velocity[:, 0, 0]
-    flat = jnp.pad(cells, ((0, 0), (0, 0), (0, ROW_PAD - cells.shape[-1])))
-    parcel = source_divergence(flat, source_safe, row_factor, codes, groups)
+    parcel = source_divergence(velocity[:, 0, 0], source_safe, row_factor, codes, groups)
 
     arrived = lax.all_to_all(parcel, ("bulk", "own"), split_axis=0, concat_axis=0, tiled=True)
     piece_w = BOX * FACE // groups

time: 103 us -> 101 us (0.981)
  local copies, waits for them, and re-layouts: 13.4 us -> 10.5 us
    pad x1, local copies, waits for them, and re-layouts: 6.24 us -> 1.55 us  [source_divergence(): spanwise = jnp.pad(cells[1], ((0, 0), (0, ROW_PAD - cells.shape[-1])))]
    squeeze x0 -> x1, local copies, waits for them, and re-layouts: none -> 1.81 us  [source_divergence(): spanwise = jnp.pad(cells[1], ((0, 0), (0, ROW_PAD - cells.shape[-1])))]
where the time goes in v8:
time: 101 us
  blocking collectives  64.6 us (64%)
  Pallas kernels  18.5 us (18%)
  local copies, waits for them, and re-layouts  10.5 us (10%)
  other arithmetic  5.6 us (6%)
  between operations  1.37 us (1%)
    all_to_all x1, blocking collectives, body(): lax.all_to_all(parcel, ('bulk', 'own'), split_axis=0, concat_axis=0, tile...  64.6 us
    pallas_call x1, Pallas kernels, source_divergence(): pl.pallas_call(divergence_kernel, in_specs=[pl.BlockSpec(memory_space=plt...  12.8 us
    pallas_call x1, Pallas kernels, line_spectra(): pl.pallas_call(dft_kernel, out_shape=(out, out), cost_estimate=pl.CostEst...  5.65 us
    all_to_all x1, local copies, waits for them, and re-layouts, body(): lax.all_to_all(parcel, ('bulk', 'own'), split_axis=0, concat_axis=0, tile...  3.21 us

profile of v8, /device:TPU:1, one launch (start us, length us, event | category | flops | bytes accessed | tf_op | source)
XLA Modules:
  0.0 100.5 jit_solution(6750134657319350307)
XLA Ops:
  1.3 0.7 add_bitcast_fusion
  2.0 0.7 fusion.2
  2.6 0.9 convert_reduce_fusion
  3.6 0.7 add_select_fusion
  4.2 0.1 select_reduce_fusion.2
  4.3 0.7 select_reduce_fusion.1
  5.0 0.1 sub.6
  5.1 0.6 gather_fusion
  5.8 0.1 copy.22
  5.8 1.8 %slice_bitcast_fusion = f32[96,5832]{1,0:T(8,128)S(1)} fusion(f32[3,1,1,96,5832]{4,3,2,1,0:T(8,128)} %param.16), kind=kLoop, calls=%fused_computation.2 | loop fusion | bytes 4478976 | tf_op jit(solution)/shard_map/squeeze | solution.py:139
  7.6 1.5 %pad.4.v_hbm = f32[96,6016]{1,0:T(8,128)} pad(f32[96,5832]{1,0:T(8,128)S(1)} %slice_bitcast_fusion, f32[]{:T(128)} %constant.30.clone.1), padding=0_0x0_184 | pad | bytes 4549636 | tf_op jit(solution)/shard_map/jit(_pad)/pad | solution.py:139
  9.2 0.6 convert_bitcast_fusion.code_ref
  9.8 0.7 broadcast_in_dim.123.fac_ref
  10.5 12.8 %shard_map.167 = f32[256,1664]{1,0:T(8,128)} custom-call(s32[96]{0:T(128)} %get-tuple-element.7.src_ref, f32[3,96,5832]{2,1,0:T(8,128)} %bitcast.23, f32[96,6016]{1,0:T(8,128)} %pad.4.v_hbm, bf16[384,256]{1,0:T(8,128)(2,1)} %constant.81.clone.sel_ref, f32[96,256]{1,0:T(8,128)} %broadcast_in_dim.123.fac_ref, f32[32,128]{1,0:T(8,128)} %convert_bitcast_fusion.code_ref), custom_call_target="tpu_custom_call" | custom-call | flops 905969664 | bytes 8634368 | tf_op jit(solution)/shard_map/pallas_call | solution.py:141
  23.4 3.2 %copy.23 = f32[256,1,1664]{2,1,0:T(1,128)S(1)} copy(f32[256,1,1664]{2,0,1:T(8,128)} %bitcast.27) | data formatting | bytes 3407872 | tf_op jit(solution)/shard_map/all_to_all | solution.py:279
  26.6 64.6 %all_to_all.12 = f32[256,1,1664]{2,1,0:T(1,128)S(1)} all-to-all(f32[256,1,1664]{2,1,0:T(1,128)S(1)} %copy.23), channel_id=1, replica_groups=mesh['bulk'=8,'own'=32] {'bulk','own'}, dimensions={0} | all-to-all | bytes 3407872 | tf_op jit(solution)/shard_map/all_to_all | solution.py:279
  91.1 0.1 copy.26
  91.3 0.2 slice.18
  91.5 0.2 select_n.95
  91.7 0.2 select_reduce_fusion
  91.9 0.3 reshape.117
  92.3 1.6 %gather_fusion.1 = f32[384,512]{1,0:T(8,128)S(1)} fusion(f32[768,512]{1,0:T(8,128)S(1)} %reshape.117, s32[1024]{0:T(1024)S(1)} %pad_clamp_fusion), kind=kCustom, calls=%fused_computation.1 | custom fusion | bytes 1574400 | tf_op jit(solution)/shard_map/jit(_take)/gather | solution.py:289
  93.9 1.0 broadcast_select_fusion.x_ref
  94.9 5.6 %shard_map.168 = (f32[32,3072]{1,0:T(8,128)}, f32[32,3072]{1,0:T(8,128)}) custom-call(f32[384,512]{1,0:T(8,128)} %broadcast_select_fusion.x_ref, bf16[384,384]{1,0:T(8,128)(2,1)} %constant.82.clone.c1h, bf16[384,384]{1,0:T(8,128)(2,1)} %constant.83.clone.c1l, bf16[384,384]{1,0:T(8,128)(2,1)} %constant.84.clone.s1h, bf16[384,384]{1,0:T(8,128)(2,1)} %constant.85.clone.s1l, ...), custom_call_target="tpu_custom_call" | custom-call | flops 1207959552 | bytes 3145728 | tf_op jit(solution)/shard_map/pallas_call | solution.py:238
  (9 shorter events, 0.1 us)

commit v9 on v8

--- a/solution.py
+++ b/solution.py
@@ -79,7 +79,10 @@
     return w[:, :PLANE_PAD]
 
 
-def divergence_kernel(src_ref, x_hbm, v_hbm, sel_ref, fac_ref, code_ref, o_ref, buf_uw, buf_v, sem):
+TAIL_BASE = 5376
+
+
+def divergence_kernel(src_ref, x_hbm, tail_hbm, sel_ref, fac_ref, code_ref, o_ref, buf, buf_tail, sem):
     owners = code_ref.shape[0]
     per_pair = src_ref.shape[0] // owners
     chunk_rows = o_ref.shape[0]
@@ -91,34 +94,35 @@
     def fetch(t, slot):
         for r in range(owners):
             row = src_ref[t * owners + r]
-            for k, field in enumerate((0, 2)):
-                pltpu.make_async_copy(
-                    x_hbm.at[field, pl.ds(row, 1), :], buf_uw.at[slot, k, pl.ds(r, 1), :], sem.at[slot, 0]
-                ).start()
             pltpu.make_async_copy(
-                v_hbm.at[pl.ds(row, 1), :], buf_v.at[slot, 0, pl.ds(r, 1), :], sem.at[slot, 1]
+                x_hbm.at[:, pl.ds(row, 1), :], buf.at[slot, :, pl.ds(r, 1), :], sem.at[slot, 0]
             ).start()
+            pltpu.make_async_copy(
+                tail_hbm.at[pl.ds(row, 1), :], buf_tail.at[slot, pl.ds(r, 1), :], sem.at[slot, 1]
+            ).start()
 
     def wait(slot):
-        pltpu.make_async_copy(x_hbm.at[pl.ds(0, 2), pl.ds(0, owners), :], buf_uw.at[slot], sem.at[slot, 0]).wait()
-        pltpu.make_async_copy(v_hbm.at[pl.ds(0, owners), :], buf_v.at[slot, 0], sem.at[slot, 1]).wait()
+        pltpu.make_async_copy(x_hbm.at[:, pl.ds(0, owners), :], buf.at[slot], sem.at[slot, 0]).wait()
+        pltpu.make_async_copy(tail_hbm.at[pl.ds(0, owners), :], buf_tail.at[slot], sem.at[slot, 1]).wait()
 
     fetch(0, 0)
     for g in range(groups):
         o_ref[g * owners:(g + 1) * owners, data_w:] = code_ref[...]
     sel = sel_ref[...]
+    last = GHOST - 1
     for t in range(per_pair):
         slot = t % 2
         if t + 1 < per_pair:
             fetch(t + 1, 1 - slot)
         wait(slot)
-        uw_ref = buf_uw.at[slot]
-        v_ref = buf_v.at[slot]
-        v_planes = [_plane(v_ref, 0, p) for p in range(GHOST)]
+        x_ref = buf.at[slot]
+        v_planes = [_plane(x_ref, 1, p) for p in range(last)]
+        tail = pltpu.roll(buf_tail[slot], WINDOW - (PLANE * last - TAIL_BASE), 1)
+        v_planes.append(tail[:, :PLANE_PAD])
         pieces = []
         for i in range(BOX):
-            u = _plane(uw_ref, 0, i + 1)
-            w = _plane(uw_ref, 1, i + 1)
+            u = _plane(x_ref, 0, i + 1)
+            w = _plane(x_ref, 2, i + 1)
             along_x = pltpu.roll(u, PLANE_PAD - 1, 1) - pltpu.roll(u, 1, 1)
             along_y = v_planes[i + 2] - v_planes[i]
             along_z = pltpu.roll(w, PLANE_PAD - GHOST, 1) - pltpu.roll(w, GHOST, 1)
@@ -136,7 +140,7 @@
     owners = codes.shape[0]
     out_w = BOX * FACE // groups * (slots // owners) + CODE_W
     sel = selection_table()
-    spanwise = jnp.pad(cells[1], ((0, 0), (0, ROW_PAD - cells.shape[-1])))
+    tail = jnp.pad(cells[1, :, TAIL_BASE:], ((0, 0), (0, TAIL_BASE + WINDOW - cells.shape[-1])))
     vmem = pl.BlockSpec(memory_space=pltpu.VMEM)
     return pl.pallas_call(
         divergence_kernel,
@@ -151,8 +155,8 @@
         out_specs=vmem,
         out_shape=jax.ShapeDtypeStruct((groups * owners, out_w), F32),
         scratch_shapes=[
-            pltpu.VMEM((2, 2, owners, cells.shape[2]), F32),
-            pltpu.VMEM((2, 1, owners, ROW_PAD), F32),
+            pltpu.VMEM((2, 3, owners, cells.shape[2]), F32),
+            pltpu.VMEM((2, owners, WINDOW), F32),
             pltpu.SemaphoreType.DMA((2, 2)),
         ],
         cost_estimate=pl.CostEstimate(
@@ -160,7 +164,7 @@
             bytes_accessed=4 * (3 * slots * ROW_PAD + groups * owners * out_w),
             transcendentals=0,
         ),
-    )(source, cells, spanwise, sel, jnp.broadcast_to(factor[:, None], (slots, FACE)), codes)
+    )(source, cells, tail, sel, jnp.broadcast_to(factor[:, None], (slots, FACE)), codes)
 
 
 def _split_np(t):

time: 101 us -> 97.8 us (0.968)
  local copies, waits for them, and re-layouts: 10.5 us -> 8.82 us
where the time goes in v9:
time: 97.8 us; the launch traced here: 97.5 us
  blocking collectives  63.6 us (65%)
  Pallas kernels  18 us (18%)
  local copies, waits for them, and re-layouts  8.82 us (9%)
  other arithmetic  5.6 us (6%)
  between operations  1.37 us (1%)
    all_to_all x1, blocking collectives, body(): lax.all_to_all(parcel, ('bulk', 'own'), split_axis=0, concat_axis=0, tile...  63.6 us
    pallas_call x1, Pallas kernels, source_divergence(): pl.pallas_call(divergence_kernel, in_specs=[pl.BlockSpec(memory_space=plt...  12.4 us
    pallas_call x1, Pallas kernels, line_spectra(): pl.pallas_call(dft_kernel, out_shape=(out, out), cost_estimate=pl.CostEst...  5.65 us
    all_to_all x1, local copies, waits for them, and re-layouts, body(): lax.all_to_all(parcel, ('bulk', 'own'), split_axis=0, concat_axis=0, tile...  3.21 us

profile of v9, /device:TPU:1, one launch (start us, length us, event | category | flops | bytes accessed | tf_op | source)
XLA Modules:
  0.0 97.5 jit_solution(11170612897666572562)
XLA Ops:
  1.3 0.7 add_bitcast_fusion
  2.0 0.7 fusion.2
  2.6 0.9 convert_reduce_fusion
  3.6 0.7 add_select_fusion
  4.2 0.1 select_reduce_fusion.2
  4.3 0.7 select_reduce_fusion.1
  5.0 0.1 sub.6
  5.1 0.6 gather_fusion
  5.8 0.1 copy.22
  5.8 1.0 slice_bitcast_fusion
  6.8 0.7 pad.4.tail_hbm
  7.5 0.6 convert_bitcast_fusion.code_ref
  8.1 0.7 broadcast_in_dim.123.fac_ref
  8.8 12.4 %shard_map.167 = f32[256,1664]{1,0:T(8,128)} custom-call(s32[96]{0:T(128)} %get-tuple-element.7.src_ref, f32[3,96,5832]{2,1,0:T(8,128)} %bitcast.25, f32[96,512]{1,0:T(8,128)} %pad.4.tail_hbm, bf16[384,256]{1,0:T(8,128)(2,1)} %constant.81.clone.sel_ref, f32[96,256]{1,0:T(8,128)} %broadcast_in_dim.123.fac_ref, f32[32,128]{1,0:T(8,128)} %convert_bitcast_fusion.code_ref), custom_call_target="tpu_custom_call" | custom-call | flops 905969664 | bytes 8634368 | tf_op jit(solution)/shard_map/pallas_call | solution.py:145
  21.2 3.2 %copy.23 = f32[256,1,1664]{2,1,0:T(1,128)S(1)} copy(f32[256,1,1664]{2,0,1:T(8,128)} %bitcast.26) | data formatting | bytes 3407872 | tf_op jit(solution)/shard_map/all_to_all | solution.py:283
  24.4 63.6 %all_to_all.12 = f32[256,1,1664]{2,1,0:T(1,128)S(1)} all-to-all(f32[256,1,1664]{2,1,0:T(1,128)S(1)} %copy.23), channel_id=1, replica_groups=mesh['bulk'=8,'own'=32] {'bulk','own'}, dimensions={0} | all-to-all | bytes 3407872 | tf_op jit(solution)/shard_map/all_to_all | solution.py:283
  88.0 0.1 copy.26
  88.2 0.2 slice.18
  88.4 0.2 select_n.95
  88.6 0.2 select_reduce_fusion
  88.8 0.3 reshape.115
  89.2 1.6 %gather_fusion.1 = f32[384,512]{1,0:T(8,128)S(1)} fusion(f32[768,512]{1,0:T(8,128)S(1)} %reshape.115, s32[1024]{0:T(1024)S(1)} %pad_clamp_fusion), kind=kCustom, calls=%fused_computation.1 | custom fusion | bytes 1574400 | tf_op jit(solution)/shard_map/jit(_take)/gather | solution.py:293
  90.8 1.0 %broadcast_select_fusion.x_ref = f32[384,512]{1,0:T(8,128)} fusion(f32[384,512]{1,0:T(8,128)S(1)} %gather_fusion.1, pred[384]{0:T(512)(128)(4,1)S(1)} %compare_and_fusion), kind=kLoop, calls=%fused_computation.5 | loop fusion | flops 196608 | bytes 1573248 | tf_op jit(solution)/shard_map/jit(_take)/select_n | solution.py:293
  91.8 5.6 %shard_map.168 = (f32[32,3072]{1,0:T(8,128)}, f32[32,3072]{1,0:T(8,128)}) custom-call(f32[384,512]{1,0:T(8,128)} %broadcast_select_fusion.x_ref, bf16[384,384]{1,0:T(8,128)(2,1)} %constant.82.clone.c1h, bf16[384,384]{1,0:T(8,128)(2,1)} %constant.83.clone.c1l, bf16[384,384]{1,0:T(8,128)(2,1)} %constant.84.clone.s1h, bf16[384,384]{1,0:T(8,128)(2,1)} %constant.85.clone.s1l, ...), custom_call_target="tpu_custom_call" | custom-call | flops 1207959552 | bytes 3145728 | tf_op jit(solution)/shard_map/pallas_call | solution.py:242
  (9 shorter events, 0.1 us)

commit v10 on v9

--- a/solution.py
+++ b/solution.py
@@ -290,7 +290,7 @@
     block_ids = jnp.arange(total_blocks, dtype=jnp.int32)
     chosen = jnp.sum(jnp.where(place_at[None, :] == block_ids[:, None], arrived_ids[None, :], 0), axis=1)
     pieces = arrived[:, :data_w].reshape(-1, piece_w)
-    cosine, sine_vals = line_spectra(jnp.take(pieces, chosen, axis=0))
+    cosine, sine_vals = line_spectra(jnp.take(pieces, chosen, axis=0, mode="clip"))
     return (cosine[None], sine_vals[None])
 
 

time: 97.8 us -> 97.3 us (level)
  other arithmetic: 5.6 us -> 4.57 us
    select_n x2 -> x0, other arithmetic: 1.02 us -> none  [body(): cosine, sine_vals = line_spectra(jnp.take(pieces, chosen, axis=0))]
where the time goes in v10:
time: 97.3 us; the launch traced here: 97 us
  blocking collectives  63.5 us (65%)
  Pallas kernels  18.1 us (19%)
  local copies, waits for them, and re-layouts  9.44 us (10%)
  other arithmetic  4.57 us (5%)
  between operations  1.36 us (1%)
    all_to_all x1, blocking collectives, body(): lax.all_to_all(parcel, ('bulk', 'own'), split_axis=0, concat_axis=0, tile...  63.5 us
    pallas_call x1, Pallas kernels, source_divergence(): pl.pallas_call(divergence_kernel, in_specs=[pl.BlockSpec(memory_space=plt...  12.5 us
    pallas_call x1, Pallas kernels, line_spectra(): pl.pallas_call(dft_kernel, out_shape=(out, out), cost_estimate=pl.CostEst...  5.65 us
    all_to_all x1, local copies, waits for them, and re-layouts, body(): lax.all_to_all(parcel, ('bulk', 'own'), split_axis=0, concat_axis=0, tile...  3.21 us
    gather x1, local copies, waits for them, and re-layouts, body(): jnp.take(pieces, chosen, axis=0, mode='clip')  2.24 us

profile of v10, /device:TPU:1, one launch (start us, length us, event | category | flops | bytes accessed | tf_op | source)
XLA Modules:
  0.0 97.0 jit_solution(1784965401706640350)
XLA Ops:
  1.3 0.7 add_bitcast_fusion
  2.0 0.7 fusion.1
  2.6 0.9 convert_reduce_fusion
  3.6 0.7 add_select_fusion
  4.2 0.1 select_reduce_fusion.2
  4.3 0.7 select_reduce_fusion.1
  5.0 0.1 sub.6
  5.1 0.6 gather_fusion
  5.8 0.1 copy.22
  5.8 1.0 slice_bitcast_fusion
  6.8 0.7 pad.4.tail_hbm
  7.5 0.6 convert_bitcast_fusion.code_ref
  8.1 0.7 broadcast_in_dim.117.fac_ref
  8.8 12.5 %shard_map.167 = f32[256,1664]{1,0:T(8,128)} custom-call(s32[96]{0:T(128)} %get-tuple-element.7.src_ref, f32[3,96,5832]{2,1,0:T(8,128)} %bitcast.25, f32[96,512]{1,0:T(8,128)} %pad.4.tail_hbm, bf16[384,256]{1,0:T(8,128)(2,1)} %constant.66.clone.sel_ref, f32[96,256]{1,0:T(8,128)} %broadcast_in_dim.117.fac_ref, f32[32,128]{1,0:T(8,128)} %convert_bitcast_fusion.code_ref), custom_call_target="tpu_custom_call" | custom-call | flops 905969664 | bytes 8634368 | tf_op jit(solution)/shard_map/pallas_call | solution.py:145
  21.3 3.2 %copy.23 = f32[256,1,1664]{2,1,0:T(1,128)S(1)} copy(f32[256,1,1664]{2,0,1:T(8,128)} %bitcast.26) | data formatting | bytes 3407872 | tf_op jit(solution)/shard_map/all_to_all | solution.py:283
  24.5 63.5 %all_to_all.12 = f32[256,1,1664]{2,1,0:T(1,128)S(1)} all-to-all(f32[256,1,1664]{2,1,0:T(1,128)S(1)} %copy.23), channel_id=1, replica_groups=mesh['bulk'=8,'own'=32] {'bulk','own'}, dimensions={0} | all-to-all | bytes 3407872 | tf_op jit(solution)/shard_map/all_to_all | solution.py:283
  88.0 0.1 copy.26
  88.1 0.2 slice.17
  88.3 0.2 select_n.75
  88.5 0.2 select_reduce_fusion
  88.7 0.3 reshape.97
  89.1 2.2 %gather_fusion.1 = f32[384,512]{1,0:T(8,128)} fusion(f32[768,512]{1,0:T(8,128)S(1)} %reshape.97, s32[1024]{0:T(1024)S(1)} %pad_clamp_fusion), kind=kCustom, calls=%fused_computation.1 | custom fusion | bytes 1574400 | tf_op jit(solution)/shard_map/jit(_take)/gather | solution.py:293
  91.3 5.6 %shard_map.168 = (f32[32,3072]{1,0:T(8,128)}, f32[32,3072]{1,0:T(8,128)}) custom-call(f32[384,512]{1,0:T(8,128)} %gather_fusion.1, bf16[384,384]{1,0:T(8,128)(2,1)} %constant.67.clone.c1h, bf16[384,384]{1,0:T(8,128)(2,1)} %constant.68.clone.c1l, bf16[384,384]{1,0:T(8,128)(2,1)} %constant.69.clone.s1h, bf16[384,384]{1,0:T(8,128)(2,1)} %constant.70.clone.s1l, ...), custom_call_target="tpu_custom_call" | custom-call | flops 1207959552 | bytes 3145728 | tf_op jit(solution)/shard_map/pallas_call | solution.py:242
  (7 shorter events, 0.1 us)

commit v11 on v10

--- a/solution.py
+++ b/solution.py
@@ -127,7 +127,8 @@
             along_y = v_planes[i + 2] - v_planes[i]
             along_z = pltpu.roll(w, PLANE_PAD - GHOST, 1) - pltpu.roll(w, GHOST, 1)
             pieces.append(along_x + (along_y + along_z))
-        interior = _exact_right(jnp.concatenate(pieces, axis=0), sel)
+        hi, lo = _split2(jnp.concatenate(pieces, axis=0))
+        interior = _dot(hi, sel) + _dot(lo, sel)
         fac = fac_ref[t * owners:(t + 1) * owners, :]
         for i in range(BOX):
             g, half = divmod(i, planes_per_group)
@@ -164,7 +165,7 @@
             bytes_accessed=4 * (3 * slots * ROW_PAD + groups * owners * out_w),
             transcendentals=0,
         ),
-    )(source, cells, tail, sel, jnp.broadcast_to(factor[:, None], (slots, FACE)), codes)
+    )(source, cells, tail, sel, factor[:, None], codes)
 
 
 def _split_np(t):

time: 97.3 us -> 97.8 us (level)
  no operation moved by 1% of the time
where the time goes in v11:
time: 97.8 us; the launch traced here: 97.5 us
  blocking collectives  63.7 us (65%)
  Pallas kernels  18.4 us (19%)
  local copies, waits for them, and re-layouts  9.44 us (10%)
  other arithmetic  4.57 us (5%)
  between operations  1.36 us (1%)
    all_to_all x1, blocking collectives, body(): lax.all_to_all(parcel, ('bulk', 'own'), split_axis=0, concat_axis=0, tile...  63.7 us
    pallas_call x1, Pallas kernels, source_divergence(): pl.pallas_call(divergence_kernel, in_specs=[pl.BlockSpec(memory_space=plt...  12.8 us
    pallas_call x1, Pallas kernels, line_spectra(): pl.pallas_call(dft_kernel, out_shape=(out, out), cost_estimate=pl.CostEst...  5.65 us
    all_to_all x1, local copies, waits for them, and re-layouts, body(): lax.all_to_all(parcel, ('bulk', 'own'), split_axis=0, concat_axis=0, tile...  3.21 us
    gather x1, local copies, waits for them, and re-layouts, body(): jnp.take(pieces, chosen, axis=0, mode='clip')  2.24 us

profile of v11, /device:TPU:1, one launch (start us, length us, event | category | flops | bytes accessed | tf_op | source)
XLA Modules:
  0.0 97.5 jit_solution(679463498519322002)
XLA Ops:
  1.3 0.7 add_bitcast_fusion
  2.0 0.7 fusion.1
  2.6 0.9 convert_reduce_fusion
  3.6 0.7 add_select_fusion
  4.2 0.1 select_reduce_fusion.2
  4.3 0.7 select_reduce_fusion.1
  5.0 0.1 sub.6
  5.1 0.7 copy.26.fac_ref
  5.9 0.6 gather_fusion
  6.5 0.1 copy.25
  6.5 1.0 slice_bitcast_fusion
  7.5 0.7 pad.4.tail_hbm
  8.2 0.6 convert_bitcast_fusion.code_ref
  8.8 12.8 %shard_map.167 = f32[256,1664]{1,0:T(8,128)} custom-call(s32[96]{0:T(128)} %get-tuple-element.7.src_ref, f32[3,96,5832]{2,1,0:T(8,128)} %bitcast.26, f32[96,512]{1,0:T(8,128)} %pad.4.tail_hbm, bf16[384,256]{1,0:T(8,128)(2,1)} %constant.66.clone.sel_ref, f32[96,1]{1,0:T(8,128)} %copy.26.fac_ref, f32[32,128]{1,0:T(8,128)} %convert_bitcast_fusion.code_ref), custom_call_target="tpu_custom_call" | custom-call | flops 905969664 | bytes 8634368 | tf_op jit(solution)/shard_map/pallas_call | solution.py:146
  21.6 3.2 %copy.27 = f32[256,1,1664]{2,1,0:T(1,128)S(1)} copy(f32[256,1,1664]{2,0,1:T(8,128)} %bitcast.29) | data formatting | bytes 3407872 | tf_op jit(solution)/shard_map/all_to_all | solution.py:284
  24.8 63.7 %all_to_all.12 = f32[256,1,1664]{2,1,0:T(1,128)S(1)} all-to-all(f32[256,1,1664]{2,1,0:T(1,128)S(1)} %copy.27), channel_id=1, replica_groups=mesh['bulk'=8,'own'=32] {'bulk','own'}, dimensions={0} | all-to-all | bytes 3407872 | tf_op jit(solution)/shard_map/all_to_all | solution.py:284
  88.5 0.1 copy.30
  88.6 0.2 slice.17
  88.8 0.2 select_n.75
  89.0 0.2 select_reduce_fusion
  89.2 0.3 reshape.96
  89.6 2.2 %gather_fusion.1 = f32[384,512]{1,0:T(8,128)} fusion(f32[768,512]{1,0:T(8,128)S(1)} %reshape.96, s32[1024]{0:T(1024)S(1)} %pad_clamp_fusion), kind=kCustom, calls=%fused_computation.1 | custom fusion | bytes 1574400 | tf_op jit(solution)/shard_map/jit(_take)/gather | solution.py:294
  91.8 5.6 %shard_map.168 = (f32[32,3072]{1,0:T(8,128)}, f32[32,3072]{1,0:T(8,128)}) custom-call(f32[384,512]{1,0:T(8,128)} %gather_fusion.1, bf16[384,384]{1,0:T(8,128)(2,1)} %constant.67.clone.c1h, bf16[384,384]{1,0:T(8,128)(2,1)} %constant.68.clone.c1l, bf16[384,384]{1,0:T(8,128)(2,1)} %constant.69.clone.s1h, bf16[384,384]{1,0:T(8,128)(2,1)} %constant.70.clone.s1l, ...), custom_call_target="tpu_custom_call" | custom-call | flops 1207959552 | bytes 3145728 | tf_op jit(solution)/shard_map/pallas_call | solution.py:243
  (7 shorter events, 0.0 us)

commit v12 on v10

--- a/solution.py
+++ b/solution.py
@@ -187,12 +187,10 @@
     same_line = (row[:, None] % lines_per_block) == (col[None, :] // SUB)
     last = _angles((row[:, None] // lines_per_block) * (col[None, :] % SUB), SUB)
     return (
-        *_split_np(np.cos(stage_one)),
-        *_split_np(np.sin(stage_one)),
+        *_split_np(np.concatenate([np.cos(stage_one), np.sin(stage_one)], axis=0)),
         jnp.asarray(np.cos(twist), F32),
         jnp.asarray(np.sin(twist), F32),
-        *_split_np(np.where(same_line, np.cos(last), 0.0)),
-        *_split_np(np.where(same_line, np.sin(last), 0.0)),
+        *_split_np(np.concatenate([np.where(same_line, np.cos(last), 0.0), np.where(same_line, np.sin(last), 0.0)], axis=0)),
     )
 
 
@@ -208,15 +206,17 @@
 LANE = 128
 
 
-def dft_kernel(x_ref, c1h, c1l, s1h, s1l, twc_ref, tws_ref, bch, bcl, bsh, bsl, cos_ref, sin_ref):
+def dft_kernel(x_ref, cs1h, cs1l, twc_ref, tws_ref, bcsh, bcsl, cos_ref, sin_ref):
     xh, xl = _split2(x_ref[...])
-    y_re = _mm3(c1h[...], c1l[...], xh, xl)
-    y_im = -_mm3(s1h[...], s1l[...], xh, xl)
+    blocks = x_ref.shape[0]
+    y = _mm3(cs1h[...], cs1l[...], xh, xl)
+    y_re = y[:blocks]
+    y_im = -y[blocks:]
     twc = twc_ref[...]
     tws = tws_ref[...]
-    bc_h, bc_l, bs_h, bs_l = bch[...], bcl[...], bsh[...], bsl[...]
+    bcs_h, bcs_l = bcsh[...], bcsl[...]
+    half_rows = bcs_h.shape[0] // 2
     norm_scale = 1.0 / math.sqrt(NX)
-    blocks = x_ref.shape[0]
     lines_per_block = LANE // SUB
     for part in range(x_ref.shape[1] // LANE):
         cols = slice(part * LANE, (part + 1) * LANE)
@@ -224,8 +224,10 @@
         yi = y_im[:, cols]
         zrh, zrl = _split2(yr * twc + yi * tws)
         zih, zil = _split2(yi * twc - yr * tws)
-        x_re = _mm3(bc_h, bc_l, zrh, zrl, NT) + _mm3(bs_h, bs_l, zih, zil, NT)
-        x_neg_im = _mm3(bs_h, bs_l, zrh, zrl, NT) - _mm3(bc_h, bc_l, zih, zil, NT)
+        from_re = _mm3(bcs_h, bcs_l, zrh, zrl, NT)
+        from_im = _mm3(bcs_h, bcs_l, zih, zil, NT)
+        x_re = from_re[:half_rows] + from_im[half_rows:]
+        x_neg_im = from_re[half_rows:] - from_im[:half_rows]
         rows = slice(part * lines_per_block, (part + 1) * lines_per_block)
         for f2 in range(cos_ref.shape[1] // blocks):
             picked = slice(f2 * lines_per_block, (f2 + 1) * lines_per_block)

time: 97.3 us -> 98.1 us (level)
  blocking collectives: 63.5 us -> 64.5 us
    all_to_all x1, blocking collectives: 63.5 us -> 64.5 us  [body(): lax.all_to_all(parcel, ('bulk', 'own'), split_axis=0, concat_axis=0, tile...]
where the time goes in v12:
time: 98.1 us; the launch traced here: 97.7 us
  blocking collectives  64.5 us (66%)
  Pallas kernels  17.9 us (18%)
  local copies, waits for them, and re-layouts  9.44 us (10%)
  other arithmetic  4.57 us (5%)
  between operations  1.36 us (1%)
    all_to_all x1, blocking collectives, body(): lax.all_to_all(parcel, ('bulk', 'own'), split_axis=0, concat_axis=0, tile...  64.5 us
    pallas_call x1, Pallas kernels, source_divergence(): pl.pallas_call(divergence_kernel, in_specs=[pl.BlockSpec(memory_space=plt...  12.9 us
    pallas_call x1, Pallas kernels, line_spectra(): pl.pallas_call(dft_kernel, out_shape=(out, out), cost_estimate=pl.CostEst...  5 us
    all_to_all x1, local copies, waits for them, and re-layouts, body(): lax.all_to_all(parcel, ('bulk', 'own'), split_axis=0, concat_axis=0, tile...  3.21 us
    gather x1, local copies, waits for them, and re-layouts, body(): jnp.take(pieces, chosen, axis=0, mode='clip')  2.24 us

profile of v12, /device:TPU:1, one launch (start us, length us, event | category | flops | bytes accessed | tf_op | source)
XLA Modules:
  0.0 97.7 jit_solution(5500784643258114143)
XLA Ops:
  1.3 0.7 add_bitcast_fusion
  2.0 0.7 fusion.1
  2.6 0.9 convert_reduce_fusion
  3.6 0.7 add_select_fusion
  4.2 0.1 select_reduce_fusion.2
  4.3 0.7 select_reduce_fusion.1
  5.0 0.1 sub.6
  5.1 0.6 gather_fusion
  5.8 0.1 copy.18
  5.8 1.0 slice_bitcast_fusion
  6.8 0.7 pad.4.tail_hbm
  7.5 0.6 convert_bitcast_fusion.code_ref
  8.1 0.7 broadcast_in_dim.117.fac_ref
  8.8 12.9 %shard_map.131 = f32[256,1664]{1,0:T(8,128)} custom-call(s32[96]{0:T(128)} %get-tuple-element.7.src_ref, f32[3,96,5832]{2,1,0:T(8,128)} %bitcast.25, f32[96,512]{1,0:T(8,128)} %pad.4.tail_hbm, bf16[384,256]{1,0:T(8,128)(2,1)} %constant.58.clone.sel_ref, f32[96,256]{1,0:T(8,128)} %broadcast_in_dim.117.fac_ref, f32[32,128]{1,0:T(8,128)} %convert_bitcast_fusion.code_ref), custom_call_target="tpu_custom_call" | custom-call | flops 905969664 | bytes 8634368 | tf_op jit(solution)/shard_map/pallas_call | solution.py:145
  21.7 3.2 %copy.19 = f32[256,1,1664]{2,1,0:T(1,128)S(1)} copy(f32[256,1,1664]{2,0,1:T(8,128)} %bitcast.26) | data formatting | bytes 3407872 | tf_op jit(solution)/shard_map/all_to_all | solution.py:285
  24.9 64.5 %all_to_all.12 = f32[256,1,1664]{2,1,0:T(1,128)S(1)} all-to-all(f32[256,1,1664]{2,1,0:T(1,128)S(1)} %copy.19), channel_id=1, replica_groups=mesh['bulk'=8,'own'=32] {'bulk','own'}, dimensions={0} | all-to-all | bytes 3407872 | tf_op jit(solution)/shard_map/all_to_all | solution.py:285
  89.4 0.1 copy.22
  89.5 0.2 slice.17
  89.7 0.2 select_n.75
  89.9 0.2 select_reduce_fusion
  90.1 0.3 reshape.97
  90.5 2.2 %gather_fusion.1 = f32[384,512]{1,0:T(8,128)} fusion(f32[768,512]{1,0:T(8,128)S(1)} %reshape.97, s32[1024]{0:T(1024)S(1)} %pad_clamp_fusion), kind=kCustom, calls=%fused_computation.1 | custom fusion | bytes 1574400 | tf_op jit(solution)/shard_map/jit(_take)/gather | solution.py:295
  92.7 5.0 %shard_map.132 = (f32[32,3072]{1,0:T(8,128)}, f32[32,3072]{1,0:T(8,128)}) custom-call(f32[384,512]{1,0:T(8,128)} %gather_fusion.1, bf16[768,384]{1,0:T(8,128)(2,1)} %constant.59.clone.cs1h, bf16[768,384]{1,0:T(8,128)(2,1)} %constant.60.clone.cs1l, f32[384,128]{1,0:T(8,128)} %constant.61.clone.twc_ref, f32[384,128]{1,0:T(8,128)} %constant.62.clone.tws_ref, ...), custom_call_target="tpu_custom_call" | custom-call | flops 1207959552 | bytes 3145728 | tf_op jit(solution)/shard_map/pallas_call | solution.py:244
  (7 shorter events, 0.1 us)

commit v13 on v12

--- a/solution.py
+++ b/solution.py
@@ -164,7 +164,7 @@
             bytes_accessed=4 * (3 * slots * ROW_PAD + groups * owners * out_w),
             transcendentals=0,
         ),
-    )(source, cells, tail, sel, jnp.broadcast_to(factor[:, None], (slots, FACE)), codes)
+    )(source, cells, tail, sel, factor[:, None], codes)
 
 
 def _split_np(t):

time: 98.1 us -> 97 us (0.989)
  blocking collectives: 64.5 us -> 60.4 us
  Pallas kernels: 17.9 us -> 20.5 us
    all_to_all x1, blocking collectives: 64.5 us -> 60.4 us  [body(): lax.all_to_all(parcel, ('bulk', 'own'), split_axis=0, concat_axis=0, tile...]
    pallas_call x1, Pallas kernels: 12.9 us -> 15.5 us  [source_divergence(): pl.pallas_call(divergence_kernel, in_specs=[pl.BlockSpec(memory_space=plt...]
where the time goes in v13:
time: 97 us; the launch traced here: 96.3 us
  blocking collectives  60.4 us (62%)
  Pallas kernels  20.5 us (21%)
  local copies, waits for them, and re-layouts  9.44 us (10%)
  other arithmetic  4.57 us (5%)
  between operations  1.36 us (1%)
    all_to_all x1, blocking collectives, body(): lax.all_to_all(parcel, ('bulk', 'own'), split_axis=0, concat_axis=0, tile...  60.4 us
    pallas_call x1, Pallas kernels, source_divergence(): pl.pallas_call(divergence_kernel, in_specs=[pl.BlockSpec(memory_space=plt...  15.5 us
    pallas_call x1, Pallas kernels, line_spectra(): pl.pallas_call(dft_kernel, out_shape=(out, out), cost_estimate=pl.CostEst...  5 us
    all_to_all x1, local copies, waits for them, and re-layouts, body(): lax.all_to_all(parcel, ('bulk', 'own'), split_axis=0, concat_axis=0, tile...  3.21 us
    gather x1, local copies, waits for them, and re-layouts, body(): jnp.take(pieces, chosen, axis=0, mode='clip')  2.24 us

profile of v13, /device:TPU:1, one launch (start us, length us, event | category | flops | bytes accessed | tf_op | source)
XLA Modules:
  0.0 96.3 jit_solution(18399740654322911788)
XLA Ops:
  1.3 0.7 add_bitcast_fusion
  2.0 0.7 fusion.1
  2.6 0.9 convert_reduce_fusion
  3.6 0.7 add_select_fusion
  4.2 0.1 select_reduce_fusion.2
  4.3 0.7 select_reduce_fusion.1
  5.0 0.1 sub.6
  5.1 0.7 copy.22.fac_ref
  5.9 0.6 gather_fusion
  6.5 0.1 copy.21
  6.5 1.0 %slice_bitcast_fusion = f32[96,456]{1,0:T(8,128)S(1)} fusion(f32[3,96,5832]{2,1,0:T(8,128)} %bitcast.25), kind=kLoop, calls=%fused_computation.5 | loop fusion | bytes 350208 | tf_op jit(solution)/shard_map/squeeze | solution.py:143
  7.5 0.7 pad.4.tail_hbm
  8.2 0.6 convert_bitcast_fusion.code_ref
  8.8 15.5 %shard_map.131 = f32[256,1664]{1,0:T(8,128)} custom-call(s32[96]{0:T(128)} %get-tuple-element.7.src_ref, f32[3,96,5832]{2,1,0:T(8,128)} %bitcast.26, f32[96,512]{1,0:T(8,128)} %pad.4.tail_hbm, bf16[384,256]{1,0:T(8,128)(2,1)} %constant.58.clone.sel_ref, f32[96,1]{1,0:T(8,128)} %copy.22.fac_ref, f32[32,128]{1,0:T(8,128)} %convert_bitcast_fusion.code_ref), custom_call_target="tpu_custom_call" | custom-call | flops 905969664 | bytes 8634368 | tf_op jit(solution)/shard_map/pallas_call | solution.py:145
  24.3 3.2 %copy.23 = f32[256,1,1664]{2,1,0:T(1,128)S(1)} copy(f32[256,1,1664]{2,0,1:T(8,128)} %bitcast.29) | data formatting | bytes 3407872 | tf_op jit(solution)/shard_map/all_to_all | solution.py:285
  27.5 60.4 %all_to_all.12 = f32[256,1,1664]{2,1,0:T(1,128)S(1)} all-to-all(f32[256,1,1664]{2,1,0:T(1,128)S(1)} %copy.23), channel_id=1, replica_groups=mesh['bulk'=8,'own'=32] {'bulk','own'}, dimensions={0} | all-to-all | bytes 3407872 | tf_op jit(solution)/shard_map/all_to_all | solution.py:285
  88.0 0.1 copy.26
  88.1 0.2 slice.17
  88.3 0.2 select_n.75
  88.5 0.2 select_reduce_fusion
  88.7 0.3 reshape.96
  89.1 2.2 %gather_fusion.1 = f32[384,512]{1,0:T(8,128)} fusion(f32[768,512]{1,0:T(8,128)S(1)} %reshape.96, s32[1024]{0:T(1024)S(1)} %pad_clamp_fusion), kind=kCustom, calls=%fused_computation.1 | custom fusion | bytes 1574400 | tf_op jit(solution)/shard_map/jit(_take)/gather | solution.py:295
  91.3 5.0 %shard_map.132 = (f32[32,3072]{1,0:T(8,128)}, f32[32,3072]{1,0:T(8,128)}) custom-call(f32[384,512]{1,0:T(8,128)} %gather_fusion.1, bf16[768,384]{1,0:T(8,128)(2,1)} %constant.59.clone.cs1h, bf16[768,384]{1,0:T(8,128)(2,1)} %constant.60.clone.cs1l, f32[384,128]{1,0:T(8,128)} %constant.61.clone.twc_ref, f32[384,128]{1,0:T(8,128)} %constant.62.clone.tws_ref, ...), custom_call_target="tpu_custom_call" | custom-call | flops 1207959552 | bytes 3145728 | tf_op jit(solution)/shard_map/pallas_call | solution.py:244
  (7 shorter events, 0.0 us)
